TPU v7x, 32 devices: a whole 2x2x4 slice. The times are simulated.
32 devices in a mesh: dom: 8 (over y, x, core), head: 4 (over z).
Axes of the slice: x: 2, y: 2, z: 4, core: 2. Of those that a mesh axis runs over, the one named last changes fastest.
Arguments:
- features: bfloat16 [25, 128, 4096], P(None, None, ('dom', 'head')), may hold values from -14 to 14
- positions: float32 [3, 4096], P(None, 'dom'), may hold values from 0 to 3
- penalty: float32 [16], replicated, may hold values from 0.01 to 0.5
- qk_weight: bfloat16 [128, 2048], replicated, may hold values from -0.5 to 0.5
- value_weight: bfloat16 [5, 128, 128], replicated, may hold values from -0.5 to 0.5
- output_weight: bfloat16 [5, 128, 128], replicated, may hold values from -0.5 to 0.5
- frames: float32 [64, 25, 25], replicated, may hold values from -3 to 3, as said below
- frame_index: int32 [64], P('dom'), may hold values from 0 to 63
- neighbours: int32 [64, 8], P('dom'), may hold values from 0 to 63, as said below
- counts: int32 [64], P('dom'), may hold values from 1 to 8
- cotangent: bfloat16 [25, 128, 4096], P(None, None, ('dom', 'head')), may hold values from -6 to 6
Outputs:
- updated: bfloat16 [25, 128, 4096], P(None, None, ('dom', 'head'))
- forces: float32 [3, 4096], P(None, ('dom', 'head'))
Inputs may be any that keep to these rules, and one draw needn't show every extreme that they name: `frames`: entries outside the diagonal blocks of components of one degree are zero. `neighbours`: row b holds 8 distinct blocks (b + o) mod 64 with |o| <= 4; the slots at and beyond counts[b] are padding.
All inputs are finite; a program needn't handle non-finite values.
Results may differ from a plain program's by a relative error of at most 0.0037.
The roundings to bfloat16 on the way count: a program that leaves them out, or rounds other values in their place, can miss the bound.
Values may be sent and summed in bfloat16 or wider, within the bound.
A program may use at most 64 MiB of HBM per device.

v0:
```python
import math

import jax
import jax.numpy as jnp
from jax import lax
from jax.sharding import PartitionSpec as P

COMP = 25
LDEG = 5
HEADS = 16
ALPHA = 64
BLOCK = 64
NBR = 8
REACH = 4
NFRAME = 64


NEG_FILL = -1e30


def extended(shard, sides, width):
    for axis, dim in sides:
        peers, length = (lax.axis_size(axis), shard.shape[dim])
        up = [(i, (i + 1) % peers) for i in range(peers)]
        down = [(j, i) for i, j in up]
        last = lax.slice_in_dim(shard, length - width, length, axis=dim)
        initial = lax.slice_in_dim(shard, 0, width, axis=dim)
        before = lax.ppermute(last, axis, up)
        after = lax.ppermute(initial, axis, down)
        shard = jnp.concatenate([before, shard, after], axis=dim)
    return shard


def from_behind(shard, axis, by):
    peers = lax.axis_size(axis)
    return lax.ppermute(shard, axis, [(i, (i + by) % peers) for i in range(peers)])


def degree_table():
    components = jnp.arange(COMP)
    degrees = jnp.sum(
        (components[:, None] >= (jnp.arange(1, LDEG) ** 2)[None, :]).astype(jnp.int32), axis=1
    )
    orders = components - degrees * degrees - degrees
    return (jnp.abs(orders) <= 2).astype(jnp.float32)


def projectors(frames):
    kept_mask = degree_table()
    return jnp.einsum("fji,j,fjk->fik", frames, kept_mask, frames, precision=lax.Precision.HIGHEST)


def mix_degrees(operand, weights, reverse):
    pieces = []
    for degree in range(weights.shape[0]):
        sliced = operand[degree * degree : (degree + 1) * (degree + 1)]
        if reverse:
            pieces.append(
                jnp.einsum(
                    "koa,co->kca", sliced, weights[degree], preferred_element_type=jnp.float32
                )
            )
        else:
            pieces.append(
                jnp.einsum(
                    "kca,co->koa", sliced, weights[degree], preferred_element_type=jnp.float32
                )
            )
    return jnp.concatenate(pieces, 0)


def pick_group(nblocks, heads_here):
    chosen = 1
    for candidate in range(1, nblocks + 1):
        if nblocks % candidate == 0 and candidate * BLOCK * heads_here <= 512:
            chosen = candidate
    return chosen


def block_meta(neighbours, counts, frame_index, projections, first_block, total_blocks):
    local_index = jnp.mod(neighbours - first_block + REACH, total_blocks)
    usable = jnp.arange(NBR)[None, :] < counts[:, None]
    onehot = (frame_index[:, None] == jnp.arange(NFRAME)[None, :]).astype(jnp.float32)
    matrices = jnp.dot(
        onehot, projections.reshape(NFRAME, COMP * COMP), precision=lax.Precision.HIGHEST
    )
    return (local_index, usable, matrices.reshape(-1, COMP, COMP))


def attend(
    queries,
    keys_ext,
    values_ext,
    grads,
    own_points,
    ext_points,
    penalty_here,
    local_index,
    usable,
    matrices,
):
    heads_here = penalty_here.shape[0]
    head_width = values_ext.shape[1] // heads_here
    query_blocks_count = queries.shape[1] // BLOCK
    ext_blocks = keys_ext.shape[1] // BLOCK
    query_blocks = queries.reshape(heads_here, ALPHA, query_blocks_count, BLOCK)
    key_blocks = keys_ext.reshape(heads_here, ALPHA, ext_blocks, BLOCK)
    value_blocks = values_ext.reshape(COMP, heads_here, head_width, ext_blocks, BLOCK)
    grad_blocks = grads.reshape(COMP, heads_here, head_width, query_blocks_count, BLOCK)
    own_blocks = own_points.reshape(3, query_blocks_count, BLOCK)
    ext_point_blocks = ext_points.reshape(3, ext_blocks, BLOCK)
    group_size = pick_group(query_blocks_count, heads_here)
    inverse_root = 1.0 / math.sqrt(ALPHA)
    block_range = jnp.arange(ext_blocks)

    def group_step(state_now, begin_at):
        attended_all, query_forces, ghost_forces = state_now
        slot_blocks = lax.dynamic_slice_in_dim(local_index, begin_at, group_size, 0)
        query_group = lax.dynamic_slice_in_dim(query_blocks, begin_at, group_size, 2)
        key_group = jnp.take(key_blocks, slot_blocks, axis=2)
        value_group = jnp.take(value_blocks, slot_blocks, axis=3)
        grad_group = lax.dynamic_slice_in_dim(grad_blocks, begin_at, group_size, 3)
        query_points = lax.dynamic_slice_in_dim(own_blocks, begin_at, group_size, 1)
        key_points = jnp.take(ext_point_blocks, slot_blocks, axis=1)
        live_slots = lax.dynamic_slice_in_dim(usable, begin_at, group_size, 0)
        group_mats = lax.dynamic_slice_in_dim(matrices, begin_at, group_size, 0)
        scores = (
            jnp.einsum(
                "hagi,hagsj->hgisj", query_group, key_group, preferred_element_type=jnp.float32
            )
            * inverse_root
        )
        separation = query_points[:, :, :, None, None] - key_points[:, :, None, :, :]
        distance = jnp.sum(separation * separation, axis=0)
        logits = scores - penalty_here[:, None, None, None, None] * distance[None]
        slot_mask = live_slots[None, :, None, :, None]
        logits = jnp.where(slot_mask, logits, NEG_FILL)
        peaks = jnp.max(logits, axis=(3, 4), keepdims=True)
        exponent = jnp.where(slot_mask, jnp.exp(logits - peaks), 0.0)
        attention = exponent / jnp.sum(exponent, axis=(3, 4), keepdims=True)
        rounded = attention.astype(jnp.bfloat16)
        aggregate = jnp.einsum(
            "hgisj,khdgsj->khdgi", rounded, value_group, preferred_element_type=jnp.float32
        )
        attended = jnp.einsum(
            "gkl,lhdgi->khdgi", group_mats, aggregate, precision=lax.Precision.HIGHEST
        ).astype(jnp.bfloat16)
        rotated = jnp.einsum(
            "glk,lhdgi->khdgi",
            group_mats,
            grad_group.astype(jnp.float32),
            precision=lax.Precision.HIGHEST,
        ).astype(jnp.bfloat16)
        weight_grads = jnp.einsum(
            "khdgi,khdgsj->hgisj", rotated, value_group, preferred_element_type=jnp.float32
        )
        logit_grads = attention * (
            weight_grads - jnp.sum(attention * weight_grads, axis=(3, 4), keepdims=True)
        )
        total = jnp.sum(2.0 * penalty_here[:, None, None, None, None] * logit_grads, axis=0)
        force_query = jnp.sum(total[None] * separation, axis=(3, 4))
        force_key = -jnp.sum(total[None] * separation, axis=2)
        onehot = (slot_blocks[:, :, None] == block_range[None, None, :]).astype(jnp.float32)
        ghost_forces = ghost_forces + jnp.einsum(
            "gse,cgsj->cej", onehot, force_key, precision=lax.Precision.HIGHEST
        )
        attended_all = lax.dynamic_update_slice_in_dim(attended_all, attended, begin_at, 3)
        query_forces = lax.dynamic_update_slice_in_dim(query_forces, force_query, begin_at, 1)
        return ((attended_all, query_forces, ghost_forces), None)

    initial = (
        jnp.zeros((COMP, heads_here, head_width, query_blocks_count, BLOCK), jnp.bfloat16),
        jnp.zeros((3, query_blocks_count, BLOCK), jnp.float32),
        jnp.zeros((3, ext_blocks, BLOCK), jnp.float32),
    )
    begins = jnp.arange(0, query_blocks_count, group_size)
    final_state, unused_out = lax.scan(group_step, initial, begins)
    attended_all, query_forces, ghost_forces = final_state
    return (
        attended_all.reshape(COMP, heads_here * head_width, query_blocks_count * BLOCK),
        query_forces.reshape(3, query_blocks_count * BLOCK),
        ghost_forces.reshape(3, ext_blocks * BLOCK),
    )


def on_device(
    features,
    positions,
    penalty,
    qk_weight,
    value_weight,
    output_weight,
    frames,
    frame_index,
    neighbours,
    counts,
    cotangent,
):
    atoms_here = features.shape[2]
    halo_width = REACH * BLOCK
    query_rows = HEADS * ALPHA
    projections = projectors(frames)
    grads = mix_degrees(cotangent, output_weight, True).astype(jnp.bfloat16)
    pos_ext = extended(positions, (("dom", 1),), halo_width)
    dom_atoms = positions.shape[1]
    dom_blocks = dom_atoms // BLOCK
    dom_count = lax.axis_size("dom")
    head_count = lax.axis_size("head")
    queries_keys = lax.dot_general(
        qk_weight, features[0], (((0,), (0,)), ((), ())), preferred_element_type=jnp.float32
    ).astype(jnp.bfloat16)
    values = mix_degrees(features, value_weight, False).astype(jnp.bfloat16)
    heads_here = HEADS // head_count
    paired = queries_keys.reshape(2, query_rows, atoms_here)
    paired_heads, values_heads, grads_heads = (
        lax.all_to_all(paired, "head", split_axis=1, concat_axis=2, tiled=True),
        lax.all_to_all(values, "head", split_axis=1, concat_axis=2, tiled=True),
        lax.all_to_all(grads, "head", split_axis=1, concat_axis=2, tiled=True),
    )
    packed = jnp.concatenate([paired_heads[1], values_heads.reshape(-1, dom_atoms)], 0)
    packed_ext = extended(packed, (("dom", 1),), halo_width)
    key_rows = heads_here * ALPHA
    penalty_here = lax.dynamic_slice_in_dim(
        penalty, lax.axis_index("head") * heads_here, heads_here
    )
    local_index, usable, matrices = block_meta(
        neighbours,
        counts,
        frame_index,
        projections,
        lax.axis_index("dom") * dom_blocks,
        dom_count * dom_blocks,
    )
    attended_all, force_query, force_ext = attend(
        paired_heads[0],
        packed_ext[:key_rows],
        packed_ext[key_rows:].reshape(COMP, -1, dom_atoms + 2 * halo_width),
        grads_heads,
        pos_ext[:, halo_width : halo_width + dom_atoms],
        pos_ext,
        penalty_here,
        local_index,
        usable,
        matrices,
    )
    attended_atoms = lax.all_to_all(attended_all, "head", split_axis=2, concat_axis=1, tiled=True)
    force_dom = force_query + force_ext[:, halo_width : halo_width + dom_atoms]
    for offset in (-1, 1):
        if offset < 0:
            rim_part = force_ext[:, :halo_width]
        else:
            rim_part = force_ext[:, halo_width + dom_atoms :]
        arrived = from_behind(rim_part, "dom", offset)
        if offset < 0:
            force_dom = force_dom.at[:, dom_atoms - halo_width :].add(arrived)
        else:
            force_dom = force_dom.at[:, :halo_width].add(arrived)
    forces = lax.psum_scatter(force_dom, "head", scatter_dimension=1, tiled=True)
    updated = (
        features.astype(jnp.float32) + mix_degrees(attended_atoms, output_weight, False)
    ).astype(jnp.bfloat16)
    return (updated, forces)


def solution(mesh):
    in_specs = (
        P(None, None, ("dom", "head")),
        P(None, "dom"),
        P(),
        P(),
        P(),
        P(),
        P(),
        P("dom"),
        P("dom", None),
        P("dom"),
        P(None, None, ("dom", "head")),
    )
    out_specs = (P(None, None, ("dom", "head")), P(None, ("dom", "head")))
    return jax.shard_map(
        on_device, mesh=mesh, in_specs=in_specs, out_specs=out_specs, check_vma=False
    )
```

profile of v0, /device:TPU:0, one launch (start us, length us, event | category | flops | bytes accessed | tf_op | source)
XLA Modules:
  0.0 372.4 jit_solution(10311147214418356075)
XLA Ops:
  10.7 6.3 %all-to-all-start = ((bf16[2,1024,128]{2,0,1:T(2,128)(2,1)}), bf16[2,1024,128]{2,0,1:T(2,128)(2,1)S(1)}, u32[]{:S(2)}, u32[]{:S(2)}) async-start(bf16[2,1024,128]{2,0,1:T(2,128)(2,1)} %copy.174), calls=%async_computation | async-start | bytes 1048576 | tf_op jit(solution)/shard_map/all_to_all | solution.py:216
  17.1 2.6 collective-permute-start.3
  23.3 8.2 %all-to-all-done = bf16[2,1024,128]{2,0,1:T(2,128)(2,1)S(1)} async-done(((bf16[2,1024,128]{2,0,1:T(2,128)(2,1)}), bf16[2,1024,128]{2,0,1:T(2,128)(2,1)S(1)}, u32[]{:S(2)}, u32[]{:S(2)}) %all-to-all-start) | async-done | bytes 524320 | tf_op jit(solution)/shard_map/all_to_all | solution.py:216
  31.5 4.3 %all-to-all-start.1 = ((bf16[25,128,128]{2,0,1:T(8,128)(2,1)}), bf16[25,128,128]{2,0,1:T(8,128)(2,1)}, u32[]{:S(2)}, u32[]{:S(2)}) async-start(bf16[25,128,128]{2,0,1:T(8,128)(2,1)} %copy.181), calls=%async_computation.1 | async-start | bytes 2097152 | tf_op jit(solution)/shard_map/all_to_all | solution.py:217
  40.6 2.4 convolution_bitcast_fusion.1
  43.0 18.1 %all-to-all-done.1 = bf16[25,128,128]{2,0,1:T(8,128)(2,1)} async-done(((bf16[25,128,128]{2,0,1:T(8,128)(2,1)}), bf16[25,128,128]{2,0,1:T(8,128)(2,1)}, u32[]{:S(2)}, u32[]{:S(2)}) %all-to-all-start.1) | async-done | bytes 819232 | tf_op jit(solution)/shard_map/all_to_all | solution.py:217
  61.1 3.5 all-to-all-start.2
  68.9 2.6 collective-permute-start.1
  78.3 11.6 %all-to-all-done.2 = bf16[25,128,128]{2,0,1:T(8,128)(2,1)S(1)} async-done(((bf16[25,128,128]{2,0,1:T(8,128)(2,1)}), bf16[25,128,128]{2,0,1:T(8,128)(2,1)S(1)}, u32[]{:S(2)}, u32[]{:S(2)}) %all-to-all-start.2) | async-done | bytes 819232 | tf_op jit(solution)/shard_map/all_to_all | solution.py:218
  95.8 3.4 reshape_reshape.3
  99.2 5.2 %copy.190 = bf16[25,4,8,16,64]{4,2,3,1,0:T(8,128)(2,1)} copy(bf16[25,4,8,16,64]{4,3,2,1,0:T(8,128)(2,1)} %reshape_reshape.3) | data formatting | bytes 3276800
  106.0 200.0 %while.17 = (s32[]{:T(128)}, bf16[25,4,8,8,64]{4,3,2,1,0:T(8,128)(2,1)}, f32[3,8,64]{2,1,0:T(8,128)S(1)}, f32[3,16,64]{2,1,0:T(8,128)S(1)}, s32[4]{0:T(128)S(1)}...) while((s32[]{:T(128)}, ...), condition=%wide.region_9.10_spmd.clone, body=%wide.region_1.9_spmd.clone.sunk | while | flops 315474432 | bytes 35243308 | solution.py:177
  118.1 5.3 %gather_fusion.2 = bf16[16,25,4,8,64]{4,3,2,1,0:T(8,128)(2,1)} fusion(bf16[25,4,8,16,64]{4,2,3,1,0:T(8,128)(2,1)} %get-tuple-element.472, s32[1024]{0:T(1024)S(1)} %pad_clamp_fusion.2), kind=kCustom, calls=%fused_computation.clone.clone.1 | custom fusion | bytes 3276864 | tf_op jit(solution)/shard_map/while/body/eval_jaxpr/jit(_take)/gather | solution.py:121
  123.4 4.2 %fusion.158 = (f32[4,2,64]{2,1,0:T(2,128)S(1)}, f32[4,2,64,8,64]{2,4,3,1,0:T(8,128)S(1)}, f32[4,2,64,8,64,1]{2,4,5,3,1,0:T(8,128)S(1)}) fusion(f32[4,2,64]{2,1,0:T(2,128)S(1)} %fusion.156, f32[4,2,64]{2,1,0:T(2,128)S(1)} %get-tuple-element.422, f32[2,64,8,64]{1,3,2,0:T(8,128)S(1)} %copy.287, f32[4]{0:T(128)S(1)} %get-tuple-element.476, ...), kind=kOutput, calls=%fused_computation.14.clone.1 | convolution fusion | flops 108035584 | bytes 5257264 | tf_op jit(solution)/shard_map/while/body/eval_jaxpr/khdgi,khdgsj->hgisj/dot_general | solution.py:154
  133.2 21.0 %dynamic_update_slice.10 = bf16[25,4,8,8,64]{4,3,2,1,0:T(8,128)(2,1)} dynamic-update-slice(bf16[25,4,8,8,64]{4,3,2,1,0:T(8,128)(2,1)} %get-tuple-element.449, bf16[25,4,8,2,64]{4,3,2,1,0:T(2,128)(2,1)S(1)} %copy.289, s32[]{:T(128)} %constant.140.clone.1..sunk, s32[]{:T(128)} %constant.140.clone.1..sunk, s32[]{:T(128)} %constant.140.clone.1..sunk, s32[]{:T(128)S(6)} %select_n.111, ...) | dynamic-update-slice | bytes 409604 | tf_op jit(solution)/shard_map/while/body/eval_jaxpr/dynamic_update_slice | solution.py:167
  168.1 5.3 %gather_fusion.2 = bf16[16,25,4,8,64]{4,3,2,1,0:T(8,128)(2,1)} fusion(bf16[25,4,8,16,64]{4,2,3,1,0:T(8,128)(2,1)} %get-tuple-element.472, s32[1024]{0:T(1024)S(1)} %pad_clamp_fusion.2), kind=kCustom, calls=%fused_computation.clone.clone.1 | custom fusion | bytes 3276864 | tf_op jit(solution)/shard_map/while/body/eval_jaxpr/jit(_take)/gather | solution.py:121
  173.4 4.2 %fusion.158 = (f32[4,2,64]{2,1,0:T(2,128)S(1)}, f32[4,2,64,8,64]{2,4,3,1,0:T(8,128)S(1)}, f32[4,2,64,8,64,1]{2,4,5,3,1,0:T(8,128)S(1)}) fusion(f32[4,2,64]{2,1,0:T(2,128)S(1)} %fusion.156, f32[4,2,64]{2,1,0:T(2,128)S(1)} %get-tuple-element.422, f32[2,64,8,64]{1,3,2,0:T(8,128)S(1)} %copy.287, f32[4]{0:T(128)S(1)} %get-tuple-element.476, ...), kind=kOutput, calls=%fused_computation.14.clone.1 | convolution fusion | flops 108035584 | bytes 5257264 | tf_op jit(solution)/shard_map/while/body/eval_jaxpr/khdgi,khdgsj->hgisj/dot_general | solution.py:154
  183.2 21.0 %dynamic_update_slice.10 = bf16[25,4,8,8,64]{4,3,2,1,0:T(8,128)(2,1)} dynamic-update-slice(bf16[25,4,8,8,64]{4,3,2,1,0:T(8,128)(2,1)} %get-tuple-element.449, bf16[25,4,8,2,64]{4,3,2,1,0:T(2,128)(2,1)S(1)} %copy.289, s32[]{:T(128)} %constant.140.clone.1..sunk, s32[]{:T(128)} %constant.140.clone.1..sunk, s32[]{:T(128)} %constant.140.clone.1..sunk, s32[]{:T(128)S(6)} %select_n.111, ...) | dynamic-update-slice | bytes 409604 | tf_op jit(solution)/shard_map/while/body/eval_jaxpr/dynamic_update_slice | solution.py:167
  218.1 5.3 %gather_fusion.2 = bf16[16,25,4,8,64]{4,3,2,1,0:T(8,128)(2,1)} fusion(bf16[25,4,8,16,64]{4,2,3,1,0:T(8,128)(2,1)} %get-tuple-element.472, s32[1024]{0:T(1024)S(1)} %pad_clamp_fusion.2), kind=kCustom, calls=%fused_computation.clone.clone.1 | custom fusion | bytes 3276864 | tf_op jit(solution)/shard_map/while/body/eval_jaxpr/jit(_take)/gather | solution.py:121
  223.4 4.2 %fusion.158 = (f32[4,2,64]{2,1,0:T(2,128)S(1)}, f32[4,2,64,8,64]{2,4,3,1,0:T(8,128)S(1)}, f32[4,2,64,8,64,1]{2,4,5,3,1,0:T(8,128)S(1)}) fusion(f32[4,2,64]{2,1,0:T(2,128)S(1)} %fusion.156, f32[4,2,64]{2,1,0:T(2,128)S(1)} %get-tuple-element.422, f32[2,64,8,64]{1,3,2,0:T(8,128)S(1)} %copy.287, f32[4]{0:T(128)S(1)} %get-tuple-element.476, ...), kind=kOutput, calls=%fused_computation.14.clone.1 | convolution fusion | flops 108035584 | bytes 5257264 | tf_op jit(solution)/shard_map/while/body/eval_jaxpr/khdgi,khdgsj->hgisj/dot_general | solution.py:154
  233.2 21.0 %dynamic_update_slice.10 = bf16[25,4,8,8,64]{4,3,2,1,0:T(8,128)(2,1)} dynamic-update-slice(bf16[25,4,8,8,64]{4,3,2,1,0:T(8,128)(2,1)} %get-tuple-element.449, bf16[25,4,8,2,64]{4,3,2,1,0:T(2,128)(2,1)S(1)} %copy.289, s32[]{:T(128)} %constant.140.clone.1..sunk, s32[]{:T(128)} %constant.140.clone.1..sunk, s32[]{:T(128)} %constant.140.clone.1..sunk, s32[]{:T(128)S(6)} %select_n.111, ...) | dynamic-update-slice | bytes 409604 | tf_op jit(solution)/shard_map/while/body/eval_jaxpr/dynamic_update_slice | solution.py:167
  268.1 5.3 %gather_fusion.2 = bf16[16,25,4,8,64]{4,3,2,1,0:T(8,128)(2,1)} fusion(bf16[25,4,8,16,64]{4,2,3,1,0:T(8,128)(2,1)} %get-tuple-element.472, s32[1024]{0:T(1024)S(1)} %pad_clamp_fusion.2), kind=kCustom, calls=%fused_computation.clone.clone.1 | custom fusion | bytes 3276864 | tf_op jit(solution)/shard_map/while/body/eval_jaxpr/jit(_take)/gather | solution.py:121
  273.4 4.2 %fusion.158 = (f32[4,2,64]{2,1,0:T(2,128)S(1)}, f32[4,2,64,8,64]{2,4,3,1,0:T(8,128)S(1)}, f32[4,2,64,8,64,1]{2,4,5,3,1,0:T(8,128)S(1)}) fusion(f32[4,2,64]{2,1,0:T(2,128)S(1)} %fusion.156, f32[4,2,64]{2,1,0:T(2,128)S(1)} %get-tuple-element.422, f32[2,64,8,64]{1,3,2,0:T(8,128)S(1)} %copy.287, f32[4]{0:T(128)S(1)} %get-tuple-element.476, ...), kind=kOutput, calls=%fused_computation.14.clone.1 | convolution fusion | flops 108035584 | bytes 5257264 | tf_op jit(solution)/shard_map/while/body/eval_jaxpr/khdgi,khdgsj->hgisj/dot_general | solution.py:154
  283.2 21.0 %dynamic_update_slice.10 = bf16[25,4,8,8,64]{4,3,2,1,0:T(8,128)(2,1)} dynamic-update-slice(bf16[25,4,8,8,64]{4,3,2,1,0:T(8,128)(2,1)} %get-tuple-element.449, bf16[25,4,8,2,64]{4,3,2,1,0:T(2,128)(2,1)S(1)} %copy.289, s32[]{:T(128)} %constant.140.clone.1..sunk, s32[]{:T(128)} %constant.140.clone.1..sunk, s32[]{:T(128)} %constant.140.clone.1..sunk, s32[]{:T(128)S(6)} %select_n.111, ...) | dynamic-update-slice | bytes 409604 | tf_op jit(solution)/shard_map/while/body/eval_jaxpr/dynamic_update_slice | solution.py:167
  306.0 3.0 reshape.147
  309.0 6.5 %copy.197 = bf16[25,32,512]{1,0,2:T(8,128)(2,1)} copy(bf16[25,32,512]{2,1,0:T(8,128)(2,1)S(1)} %reshape.147) | data formatting | bytes 1638400 | tf_op jit(solution)/shard_map/reshape | solution.py:180
  315.5 5.3 %reshape.212 = bf16[4,2,51200]{2,1,0:T(2,128)(2,1)} reshape(bf16[512,25,32]{2,1,0:T(8,128)(2,1)} %bitcast.289) | data formatting | bytes 1638400
  320.8 3.6 all-to-all-start.3
  327.7 2.6 collective-permute-done.5
  332.9 18.3 %reduce-scatter.4.cloned.1.call-done = f32[128,3]{1,0:T(8,128)} async-done(((f32[512,3]{1,0:T(8,128)}), f32[128,3]{1,0:T(8,128)}) %reduce-scatter.4.cloned.1.call-update) | async-done | bytes 1552
  352.7 4.1 %reshape.213 = bf16[512,25,32]{2,1,0:T(8,128)(2,1)} reshape(bf16[4,2,51200]{2,1,0:T(2,128)(2,1)S(1)} %all-to-all-done.3) | data formatting | bytes 1638400
  356.9 5.2 %copy.220 = bf16[25,32,4,128]{3,2,1,0:T(4,128)(2,1)S(1)} copy(bf16[25,32,4,128]{1,0,3,2:T(8,128)(2,1)} %bitcast.290) | data formatting | bytes 1638400 | tf_op jit(solution)/shard_map/all_to_all | solution.py:246
  (259 shorter events, 110.3 us)
Async XLA Ops:
  7.2 12.6 %copy-start.5 = (bf16[25,128,128]{2,1,0:T(8,128)(2,1)S(1)}, bf16[25,128,128]{2,1,0:T(8,128)(2,1)}, u32[]{:S(2)}) copy-start(bf16[25,128,128]{2,1,0:T(8,128)(2,1)} %param.17) | copy-start | bytes 2457604
  7.2 9.8 %copy-start.12 = (f32[3,512]{1,0:T(4,128)S(1)}, f32[3,512]{1,0:T(4,128)}, u32[]{:S(2)}) copy-start(f32[3,512]{1,0:T(4,128)} %param.18) | copy-start | bytes 18436
  7.2 12.5 %copy-start.11 = (bf16[5,128,128]{2,1,0:T(8,128)(2,1)S(1)}, bf16[5,128,128]{2,1,0:T(8,128)(2,1)}, u32[]{:S(2)}) copy-start(bf16[5,128,128]{2,1,0:T(8,128)(2,1)} %param.21) | copy-start | bytes 491524
  9.3 11.7 %copy-start.8 = (bf16[25,128,128]{2,1,0:T(8,128)(2,1)S(1)}, bf16[25,128,128]{2,1,0:T(8,128)(2,1)}, u32[]{:S(2)}) copy-start(bf16[25,128,128]{2,1,0:T(8,128)(2,1)} %param.27) | copy-start | bytes 2457604
  9.3 11.7 %copy-start.9 = (bf16[5,128,128]{2,1,0:T(8,128)(2,1)S(1)}, bf16[5,128,128]{2,1,0:T(8,128)(2,1)}, u32[]{:S(2)}) copy-start(bf16[5,128,128]{2,1,0:T(8,128)(2,1)} %param.22) | copy-start | bytes 491524
  10.7 20.8 %all-to-all-start = ((bf16[2,1024,128]{2,0,1:T(2,128)(2,1)}), bf16[2,1024,128]{2,0,1:T(2,128)(2,1)S(1)}, u32[]{:S(2)}, u32[]{:S(2)}) async-start(bf16[2,1024,128]{2,0,1:T(2,128)(2,1)} %copy.174), calls=%async_computation | async-start | bytes 1048576 | tf_op jit(solution)/shard_map/all_to_all | solution.py:216
  17.0 58.9 %collective-permute-start.2 = (f32[3,256]{1,0:T(4,128)S(1)}, f32[3,256]{1,0:T(4,128)S(1)}, u32[]{:S(2)}, u32[]{:S(2)}) collective-permute-start(f32[3,256]{1,0:T(4,128)S(1)} %get-tuple-element.313), channel_id=1, source_target_pairs={{0,4},{4,8},{8,12},{12,16},{16,20},{20,24},{24,28},{28,0},{1,5},{5... | collective-permute-start | bytes 9224 | tf_op jit(solution)/shard_map/ppermute | solution.py:28
  17.1 58.9 %collective-permute-start.3 = (f32[3,256]{1,0:T(4,128)S(1)}, f32[3,256]{1,0:T(4,128)S(1)}, u32[]{:S(2)}, u32[]{:S(2)}) collective-permute-start(f32[3,256]{1,0:T(4,128)S(1)} %get-tuple-element.314), channel_id=1, source_target_pairs={{4,0},{8,4},{12,8},{16,12},{20,16},{24,20},{28,24},{0,28},{5,1},{9... | collective-permute-start | bytes 9224 | tf_op jit(solution)/shard_map/ppermute | solution.py:29
  23.3 14.3 %copy-start.7 = (f32[64,25,25]{0,2,1:T(8,128)S(1)}, f32[64,25,25]{0,2,1:T(8,128)}, u32[]{:S(2)}) copy-start(f32[64,25,25]{0,2,1:T(8,128)} %param.23) | copy-start | bytes 480004
  31.5 29.6 %all-to-all-start.1 = ((bf16[25,128,128]{2,0,1:T(8,128)(2,1)}), bf16[25,128,128]{2,0,1:T(8,128)(2,1)}, u32[]{:S(2)}, u32[]{:S(2)}) async-start(bf16[25,128,128]{2,0,1:T(8,128)(2,1)} %copy.181), calls=%async_computation.1 | async-start | bytes 2097152 | tf_op jit(solution)/shard_map/all_to_all | solution.py:217
  40.6 24.0 %copy-start.13 = (s32[8,8]{1,0:T(8,128)S(1)}, s32[8,8]{1,0:T(8,128)}, u32[]{:S(2)}) copy-start(s32[8,8]{1,0:T(8,128)} %param.25) | copy-start | bytes 772
  61.1 28.8 %all-to-all-start.2 = ((bf16[25,128,128]{2,0,1:T(8,128)(2,1)}), bf16[25,128,128]{2,0,1:T(8,128)(2,1)S(1)}, u32[]{:S(2)}, u32[]{:S(2)}) async-start(bf16[25,128,128]{2,0,1:T(8,128)(2,1)} %copy.188), calls=%async_computation.2 | async-start | bytes 2097152 | tf_op jit(solution)/shard_map/all_to_all | solution.py:218
  67.7 3.9 %copy-start.15 = (s32[8]{0:T(128)S(1)}, s32[8]{0:T(128)}, u32[]{:S(2)}) copy-start(s32[8]{0:T(128)} %param.26) | copy-start | bytes 100
  67.8 6.4 %copy-start.14 = (s32[8]{0:T(128)S(1)}, s32[8]{0:T(128)}, u32[]{:S(2)}) copy-start(s32[8]{0:T(128)} %param.24) | copy-start | bytes 100
  68.9 7.0 %copy-start.16 = (f32[16]{0:T(128)S(1)}, f32[16]{0:T(128)}, u32[]{:S(2)}) copy-start(f32[16]{0:T(128)} %param.19) | copy-start | bytes 196
  68.9 23.3 %collective-permute-start = (bf16[1056,256]{1,0:T(8,128)(2,1)}, bf16[1056,256]{1,0:T(8,128)(2,1)}, u32[]{:S(2)}, u32[]{:S(2)}) collective-permute-start(bf16[1056,256]{1,0:T(8,128)(2,1)} %get-tuple-element.307), channel_id=1, source_target_pairs={{0,4},{4,8},{8,12},{12,16},{16,20},{20,24},{24,28},{28,0},{1,5},{5... | collective-permute-start | bytes 1622024 | tf_op jit(solution)/shard_map/ppermute | solution.py:28
  68.9 23.3 %collective-permute-start.1 = (bf16[1056,256]{1,0:T(8,128)(2,1)}, bf16[1056,256]{1,0:T(8,128)(2,1)}, u32[]{:S(2)}, u32[]{:S(2)}) collective-permute-start(bf16[1056,256]{1,0:T(8,128)(2,1)} %get-tuple-element.308), channel_id=1, source_target_pairs={{4,0},{8,4},{12,8},{16,12},{20,16},{24,20},{28,24},{0,28},{5,1},{9... | collective-permute-start | bytes 1622024 | tf_op jit(solution)/shard_map/ppermute | solution.py:29
  106.0 4.9 %copy-start.3 = (bf16[4,64,16,64]{3,1,2,0:T(8,128)(2,1)}, bf16[4,64,16,64]{3,1,2,0:T(8,128)(2,1)S(1)}, u32[]{:S(2)}) copy-start(bf16[4,64,16,64]{3,1,2,0:T(8,128)(2,1)S(1)} %get-tuple-element.475) | copy-start | bytes 1572868 | tf_op jit(solution)/shard_map/while
  132.7 23.2 %copy-start.4 = (bf16[4,64,16,64]{3,1,2,0:T(8,128)(2,1)S(1)}, bf16[4,64,16,64]{3,1,2,0:T(8,128)(2,1)}, u32[]{:S(2)}) copy-start(bf16[4,64,16,64]{3,1,2,0:T(8,128)(2,1)} %copy-done.3) | copy-start | bytes 1572868 | tf_op jit(solution)/shard_map/while
  156.0 4.9 %copy-start.3 = (bf16[4,64,16,64]{3,1,2,0:T(8,128)(2,1)}, bf16[4,64,16,64]{3,1,2,0:T(8,128)(2,1)S(1)}, u32[]{:S(2)}) copy-start(bf16[4,64,16,64]{3,1,2,0:T(8,128)(2,1)S(1)} %get-tuple-element.475) | copy-start | bytes 1572868 | tf_op jit(solution)/shard_map/while
  182.7 23.2 %copy-start.4 = (bf16[4,64,16,64]{3,1,2,0:T(8,128)(2,1)S(1)}, bf16[4,64,16,64]{3,1,2,0:T(8,128)(2,1)}, u32[]{:S(2)}) copy-start(bf16[4,64,16,64]{3,1,2,0:T(8,128)(2,1)} %copy-done.3) | copy-start | bytes 1572868 | tf_op jit(solution)/shard_map/while
  206.0 4.9 %copy-start.3 = (bf16[4,64,16,64]{3,1,2,0:T(8,128)(2,1)}, bf16[4,64,16,64]{3,1,2,0:T(8,128)(2,1)S(1)}, u32[]{:S(2)}) copy-start(bf16[4,64,16,64]{3,1,2,0:T(8,128)(2,1)S(1)} %get-tuple-element.475) | copy-start | bytes 1572868 | tf_op jit(solution)/shard_map/while
  232.7 23.2 %copy-start.4 = (bf16[4,64,16,64]{3,1,2,0:T(8,128)(2,1)S(1)}, bf16[4,64,16,64]{3,1,2,0:T(8,128)(2,1)}, u32[]{:S(2)}) copy-start(bf16[4,64,16,64]{3,1,2,0:T(8,128)(2,1)} %copy-done.3) | copy-start | bytes 1572868 | tf_op jit(solution)/shard_map/while
  256.0 4.9 %copy-start.3 = (bf16[4,64,16,64]{3,1,2,0:T(8,128)(2,1)}, bf16[4,64,16,64]{3,1,2,0:T(8,128)(2,1)S(1)}, u32[]{:S(2)}) copy-start(bf16[4,64,16,64]{3,1,2,0:T(8,128)(2,1)S(1)} %get-tuple-element.475) | copy-start | bytes 1572868 | tf_op jit(solution)/shard_map/while
  282.8 23.2 %copy-start.4 = (bf16[4,64,16,64]{3,1,2,0:T(8,128)(2,1)S(1)}, bf16[4,64,16,64]{3,1,2,0:T(8,128)(2,1)}, u32[]{:S(2)}) copy-start(bf16[4,64,16,64]{3,1,2,0:T(8,128)(2,1)} %copy-done.3) | copy-start | bytes 1572868 | tf_op jit(solution)/shard_map/while
  320.8 11.1 %copy-start.6 = (bf16[25,128,128]{2,1,0:T(8,128)(2,1)S(1)}, bf16[25,128,128]{2,1,0:T(8,128)(2,1)}, u32[]{:S(2)}) copy-start(bf16[25,128,128]{2,1,0:T(8,128)(2,1)} %param.17) | copy-start | bytes 2457604
  320.8 31.9 %all-to-all-start.3 = ((bf16[4,2,51200]{2,1,0:T(2,128)(2,1)}), bf16[4,2,51200]{2,1,0:T(2,128)(2,1)S(1)}, u32[]{:S(2)}, u32[]{:S(2)}) async-start(bf16[4,2,51200]{2,1,0:T(2,128)(2,1)} %reshape.212), calls=%async_computation.3 | async-start | bytes 1638400 | tf_op jit(solution)/shard_map/all_to_all | solution.py:246
  324.4 26.8 %reduce-scatter.4.cloned.1.call-start = ((), (), s32[]{:S(2)}) async-start(), calls=%async_computation.5 | async-start | bytes 327680
  325.3 2.4 collective-permute-start.4
  326.4 3.9 %collective-permute-start.5 = (f32[3,256]{1,0:T(4,128)S(1)}, f32[3,256]{1,0:T(4,128)S(1)}, u32[]{:S(2)}, u32[]{:S(2)}) collective-permute-start(f32[3,256]{1,0:T(4,128)S(1)} %get-tuple-element.311), channel_id=1, source_target_pairs={{0,4},{4,8},{8,12},{12,16},{16,20},{20,24},{24,28},{28,0},{1,5},{5... | collective-permute-start | bytes 9224 | tf_op jit(solution)/shard_map/ppermute | solution.py:36
  356.9 5.6 %copy-start.10 = (bf16[5,128,128]{2,1,0:T(8,128)(2,1)S(1)}, bf16[5,128,128]{2,1,0:T(8,128)(2,1)}, u32[]{:S(2)}) copy-start(bf16[5,128,128]{2,1,0:T(8,128)(2,1)} %param.22) | copy-start | bytes 491524
  363.5 2.0 copy-start.1
  (5 other events, 8.8 us)
Sparse Core Ops, SparseCore 0:
  332.0 19.1 reduce-scatter.3
where the time goes:
time: 375 us; the launch traced here: 372 us
  local copies, waits for them, and re-layouts  201 us (54%)
  waiting for transfers between devices  60.2 us (16%)
  matrix products  45.4 us (12%)
  starting transfers between devices  24.2 us (6%)
  other arithmetic  18.4 us (5%)
  between operations  14.6 us (4%)
  loops' own time  8.68 us (2%)
    dynamic_update_slice x8, local copies, waits for them, and re-layouts, group_step(): lax.dynamic_update_slice_in_dim(attended_all, attended, begin_at, 3)  85.9 us
    unnamed x39, local copies, waits for them, and re-layouts  21.9 us
    gather x4, local copies, waits for them, and re-layouts, group_step(): value_group = jnp.take(value_blocks, slot_blocks, axis=3)  21 us
    unnamed x2, waiting for transfers between devices  18.3 us
    all_to_all x1, waiting for transfers between devices, on_device(): lax.all_to_all(values, 'head', split_axis=1, concat_axis=2, tiled=True)  18.1 us
    dot_general x4, matrix products, group_step(): jnp.einsum('khdgi,khdgsj->hgisj', rotated, value_group, preferred_element...  16.7 us
    all_to_all x1, waiting for transfers between devices, on_device(): lax.all_to_all(grads, 'head', split_axis=1, concat_axis=2, tiled=True)  11.6 us
    reshape x2, local copies, waits for them, and re-layouts, attend(): attended_all.reshape(COMP, heads_here * head_width, query_blocks_count *...  9.53 us
  transfers between devices with their start and end apart: 11, of which 6 were waited for; matrix products, arithmetic and copies ran while one was open for 8% of the time, Pallas kernels for 0%

commit v1 on v0

v1 whole, which is shorter than its diff:
```python
import functools
import math

import jax
import jax.numpy as jnp
import numpy as np
from jax import lax
from jax.experimental import pallas as pl
from jax.experimental.pallas import tpu as pltpu
from jax.sharding import PartitionSpec as P

BLOCK = 64
REACH = 4
FAR = 1e30
VMEM_LIMIT = 40 * 1024 * 1024


def degree_of(k):
    return math.isqrt(k)


def pair_table(comp):
    pairs = []
    for k in range(comp):
        l = degree_of(k)
        for m in range(l * l, (l + 1) * (l + 1)):
            pairs.append((k, m))
    return pairs


def vmem():
    return pl.BlockSpec(memory_space=pltpu.VMEM)


def dot(a, b, ca, cb):
    return lax.dot_general(
        a, b, (((ca,), (cb,)), ((), ())), preferred_element_type=jnp.float32
    )


def values_kernel(features, weight, out):
    comp = features.shape[0]
    ranks, rows, width, atoms = out.shape
    for k in range(comp):
        mixed = dot(weight[degree_of(k)], features[k], 0, 0)
        out[:, k] = mixed.reshape(ranks, width, atoms).astype(jnp.bfloat16)
    scalars = features[0].astype(jnp.float32).reshape(rows - comp, width, atoms)
    scalars = scalars.astype(jnp.bfloat16)
    for rank in range(ranks):
        out[rank, comp:] = scalars


def back_kernel(cotangent, weight, out):
    ranks, comp, width, atoms = out.shape
    for k in range(comp):
        mixed = dot(weight[degree_of(k)], cotangent[k], 1, 0)
        out[:, k] = mixed.reshape(ranks, width, atoms).astype(jnp.bfloat16)


def update_kernel(features, attended, weight, out):
    comp, channels, atoms = out.shape
    for k in range(comp):
        gathered = attended[:, k].astype(jnp.float32).reshape(channels, atoms)
        mixed = dot(weight[degree_of(k)], gathered.astype(jnp.bfloat16), 0, 0)
        out[k] = (features[k].astype(jnp.float32) + mixed).astype(jnp.bfloat16)


def attention_kernel(
    heads,
    alpha,
    comp,
    penalty,
    before,
    own,
    after,
    back,
    q_weight,
    k_weight,
    coef,
    mask,
    points,
    points_t,
    attended,
    forces,
    values_s,
    keys_s,
    queries_s,
    rotated_s,
    aggregate_s,
):
    step = pl.program_id(0)
    tiles, _, width, atoms = own.shape
    halo = before.shape[0]
    window = 2 * halo + 1
    head_width = width // heads
    channels = q_weight.shape[0]

    def prepare(ref, at, slot, with_query):
        tile = ref[at].astype(jnp.float32)
        for h in range(heads):
            part = tile[:comp, h * head_width : (h + 1) * head_width]
            values_s[slot, h] = part.reshape(comp * head_width, atoms).astype(jnp.bfloat16)
        scalars = tile[comp:].reshape(channels, atoms)
        keys = dot(k_weight[...], scalars.astype(jnp.bfloat16), 0, 0)
        keys_s[slot] = keys.reshape(heads, alpha, atoms).astype(jnp.bfloat16)
        if with_query:
            turned = scalars.T.astype(jnp.bfloat16)
            for h in range(heads):
                queries_s[at, h] = dot(turned, q_weight[:, h * alpha : (h + 1) * alpha], 1, 0).astype(
                    jnp.bfloat16
                )

    @pl.when(step == 0)
    def _():
        forces[...] = jnp.zeros_like(forces)

        def edge(i, carry):
            prepare(before, i, i, False)
            prepare(after, i, i + halo + tiles, False)
            return carry

        def inner(i, carry):
            prepare(own, i, i + halo, True)
            return carry

        lax.fori_loop(0, halo, edge, 0)
        lax.fori_loop(0, tiles, inner, 0)

    pairs = pair_table(comp)
    index_of = {pair: n for n, pair in enumerate(pairs)}

    def rotate(source, k, turned):
        l = degree_of(k)
        total = None
        for m in range(l * l, (l + 1) * (l + 1)):
            row = index_of[(m, k) if turned else (k, m)]
            term = coef[0, row : row + 1, :] * source(m)
            total = term if total is None else total + term
        return total

    for k in range(comp):
        rotated_s[k] = (
            rotate(lambda m: back[step, m].astype(jnp.float32), k, True)
            .astype(jnp.bfloat16)
            .astype(jnp.float32)
        )

    def windowed(get):
        return jnp.concatenate([get(step + w) for w in range(window)], axis=-1)

    rows = [windowed(lambda s, c=c: points[s, c : c + 1, :]) for c in range(3)]
    columns = [points_t[step, :, c : c + 1] for c in range(3)]
    distance = None
    for c in range(3):
        apart = columns[c] - rows[c]
        distance = apart * apart if distance is None else distance + apart * apart
    per_tile = atoms // BLOCK
    hidden = jnp.concatenate(
        [
            jnp.broadcast_to(mask[0, r : r + 1, :], (BLOCK, window * atoms))
            for r in range(per_tile)
        ],
        axis=0,
    )
    distance = jnp.maximum(distance, hidden)
    total = jnp.zeros((atoms, window * atoms), jnp.float32)
    scale = 1.0 / math.sqrt(alpha)
    for h in range(heads):
        strength = penalty[h]
        keys = windowed(lambda s: keys_s[s, h])
        values = windowed(lambda s: values_s[s, h])
        logits = dot(queries_s[step, h], keys, 1, 0) * scale - strength * distance
        peaks = jnp.max(logits, axis=1, keepdims=True)
        exponent = jnp.exp(logits - peaks)
        inverse = 1.0 / jnp.sum(exponent, axis=1, keepdims=True)
        attention = exponent * inverse
        aggregate = dot(values, attention.astype(jnp.bfloat16), 1, 1)
        aggregate_s[:, h * head_width : (h + 1) * head_width] = aggregate.reshape(
            comp, head_width, atoms
        )
        turned = rotated_s[:, h * head_width : (h + 1) * head_width].reshape(comp * head_width, atoms)
        weight_grads = dot(turned.T.astype(jnp.bfloat16), values, 1, 0)
        mean = jnp.sum(attention * weight_grads, axis=1, keepdims=True)
        total = total + (2.0 * strength) * (attention * (weight_grads - mean))
    for k in range(comp):
        attended[0, k] = rotate(lambda m: aggregate_s[m], k, False).astype(jnp.bfloat16)

    lane = lax.broadcasted_iota(jnp.int32, (atoms, atoms), 1)
    mine = jnp.zeros((atoms, atoms), jnp.float32)
    theirs = []
    for c in range(3):
        weighted = total * (columns[c] - rows[c])
        mine = jnp.where(lane == c, jnp.sum(weighted, axis=1, keepdims=True), mine)
        theirs.append(jnp.sum(weighted, axis=0, keepdims=True))
    mine = mine.T
    for c in range(3):
        forces[step + halo, c : c + 1, :] = forces[step + halo, c : c + 1, :] + mine[c : c + 1]
        for w in range(window):
            forces[step + w, c : c + 1, :] = (
                forces[step + w, c : c + 1, :] - theirs[c][:, w * atoms : (w + 1) * atoms]
            )


def on_device(
    features,
    positions,
    penalty,
    qk_weight,
    value_weight,
    output_weight,
    frames,
    frame_index,
    neighbours,
    counts,
    cotangent,
):
    comp, channels, atoms = features.shape
    ranks = lax.axis_size("head")
    doms = lax.axis_size("dom")
    heads_all = penalty.shape[0]
    heads = heads_all // ranks
    alpha = qk_weight.shape[1] // (2 * heads_all)
    width = channels // ranks
    tiles = positions.shape[1] // atoms
    per_tile = atoms // BLOCK
    halo = -(-REACH * BLOCK // atoms)
    window = 2 * halo + 1
    scalar_rows = channels // width
    head_width = width // heads
    slots = tiles + 2 * halo
    up = [(i, (i + 1) % doms) for i in range(doms)]
    down = [(j, i) for i, j in up]
    rank = lax.axis_index("head")
    params = pltpu.CompilerParams(vmem_limit_bytes=VMEM_LIMIT)
    mix_cost = pl.CostEstimate(
        flops=2 * comp * channels * channels * atoms,
        bytes_accessed=4 * comp * channels * atoms,
        transcendentals=0,
    )

    packed = pl.pallas_call(
        values_kernel,
        out_shape=jax.ShapeDtypeStruct((ranks, comp + scalar_rows, width, atoms), jnp.bfloat16),
        in_specs=[vmem()] * 2,
        out_specs=vmem(),
        compiler_params=params,
        cost_estimate=mix_cost,
        name="mix_values",
    )(features, value_weight)
    own = lax.all_to_all(packed, "head", split_axis=0, concat_axis=0, tiled=True)
    before = lax.ppermute(own[tiles - halo :], "dom", up)
    after = lax.ppermute(own[:halo], "dom", down)

    grads = pl.pallas_call(
        back_kernel,
        out_shape=jax.ShapeDtypeStruct((ranks, comp, width, atoms), jnp.bfloat16),
        in_specs=[vmem()] * 2,
        out_specs=vmem(),
        compiler_params=params,
        cost_estimate=mix_cost,
        name="mix_back",
    )(cotangent, output_weight)
    back = lax.all_to_all(grads, "head", split_axis=0, concat_axis=0, tiled=True)

    reach_atoms = halo * atoms
    last = lax.ppermute(positions[:, positions.shape[1] - reach_atoms :], "dom", up)
    first = lax.ppermute(positions[:, :reach_atoms], "dom", down)
    points = jnp.concatenate([last, positions, first], axis=1)
    points = points.reshape(3, slots, atoms).transpose(1, 0, 2)
    points_t = positions.reshape(3, tiles, atoms).transpose(1, 2, 0)

    chosen = jnp.take(frames, frame_index, axis=0)
    components = np.arange(comp)
    degrees = np.array([degree_of(k) for k in components])
    keep = np.abs(components - degrees * degrees - degrees) <= 2
    pairs = np.array(pair_table(comp))
    projections = jnp.einsum(
        "fji,j,fjk->fik",
        chosen,
        jnp.asarray(keep, jnp.float32),
        chosen,
        precision=lax.Precision.HIGHEST,
    )
    flat = projections.reshape(-1, comp * comp)
    picked = jnp.take(flat, jnp.asarray(pairs[:, 0] * comp + pairs[:, 1]), axis=1)
    coef = jnp.broadcast_to(
        picked.reshape(tiles, per_tile, -1).transpose(0, 2, 1)[..., None],
        (tiles, len(pairs), per_tile, BLOCK),
    ).reshape(tiles, len(pairs), atoms)

    blocks = neighbours.shape[0]
    block_ids = lax.axis_index("dom") * blocks + jnp.arange(blocks)
    offset = jnp.mod(neighbours - block_ids[:, None] + REACH, doms * blocks)
    usable = jnp.arange(neighbours.shape[1])[None, :] < counts[:, None]
    shift = jnp.arange(blocks) % per_tile + halo * per_tile - REACH
    place = offset + shift[:, None]
    hit = jnp.any(
        usable[:, :, None] & (place[:, :, None] == jnp.arange(window * per_tile)), axis=1
    )
    mask = jnp.broadcast_to(
        jnp.where(hit, 0.0, FAR).astype(jnp.float32)[..., None],
        (blocks, window * per_tile, BLOCK),
    ).reshape(tiles, per_tile, window * atoms)

    q_weight = lax.dynamic_slice_in_dim(qk_weight, rank * heads * alpha, heads * alpha, 1)
    k_weight = lax.dynamic_slice_in_dim(
        qk_weight, (heads_all + rank * heads) * alpha, heads * alpha, 1
    )
    penalty_here = lax.dynamic_slice_in_dim(penalty, rank * heads, heads)

    attended, forces = pl.pallas_call(
        functools.partial(attention_kernel, heads, alpha, comp),
        grid=(tiles,),
        out_shape=(
            jax.ShapeDtypeStruct((tiles, comp, width, atoms), jnp.bfloat16),
            jax.ShapeDtypeStruct((slots, 3, atoms), jnp.float32),
        ),
        in_specs=[pl.BlockSpec(memory_space=pltpu.SMEM)]
        + [vmem()] * 6
        + [
            pl.BlockSpec((1, len(pairs), atoms), lambda t: (t, 0, 0)),
            pl.BlockSpec((1, per_tile, window * atoms), lambda t: (t, 0, 0)),
            vmem(),
            vmem(),
        ],
        out_specs=(
            pl.BlockSpec((1, comp, width, atoms), lambda t: (t, 0, 0, 0)),
            vmem(),
        ),
        scratch_shapes=[
            pltpu.VMEM((slots, heads, comp * head_width, atoms), jnp.bfloat16),
            pltpu.VMEM((slots, heads, alpha, atoms), jnp.bfloat16),
            pltpu.VMEM((tiles, heads, atoms, alpha), jnp.bfloat16),
            pltpu.VMEM((comp, width, atoms), jnp.float32),
            pltpu.VMEM((comp, width, atoms), jnp.float32),
        ],
        compiler_params=params,
        name="attention",
    )(
        penalty_here,
        before,
        own,
        after,
        back,
        q_weight,
        k_weight,
        coef,
        mask,
        points,
        points_t,
    )

    arrived = lax.all_to_all(attended, "head", split_axis=0, concat_axis=0, tiled=True)
    low = lax.ppermute(forces[:halo], "dom", down)
    high = lax.ppermute(forces[slots - halo :], "dom", up)
    shared = forces[halo : halo + tiles]
    shared = shared + jnp.concatenate([high, jnp.zeros_like(shared[halo:])], axis=0)
    shared = shared + jnp.concatenate([jnp.zeros_like(shared[halo:]), low], axis=0)
    shares = lax.all_to_all(shared, "head", split_axis=0, concat_axis=0, tiled=True)
    force = jnp.sum(shares, axis=0)

    updated = pl.pallas_call(
        update_kernel,
        out_shape=jax.ShapeDtypeStruct(features.shape, jnp.bfloat16),
        in_specs=[vmem()] * 3,
        out_specs=vmem(),
        compiler_params=params,
        cost_estimate=mix_cost,
        name="update",
    )(features, arrived, output_weight)
    return (updated, force)


def solution(mesh):
    split = ("dom", "head")
    in_specs = (
        P(None, None, split),
        P(None, "dom"),
        P(),
        P(),
        P(),
        P(),
        P(),
        P("dom"),
        P("dom", None),
        P("dom"),
        P(None, None, split),
    )
    out_specs = (P(None, None, split), P(None, split))
    return jax.shard_map(
        on_device, mesh=mesh, in_specs=in_specs, out_specs=out_specs, check_vma=False
    )
```

time: 375 us -> 113 us (0.30)
  local copies, waits for them, and re-layouts: 201 us -> 19.5 us
  matrix products: 45.4 us -> 0.47 us
  waiting for transfers between devices: 60.2 us -> 41.5 us
  Pallas kernels: 0 us -> 17.6 us
  other arithmetic: 18.4 us -> 2.78 us
  between operations: 14.6 us -> 0.78 us
  loops' own time: 8.68 us -> 0 us
  blocking collectives: 0 us -> 8.11 us
    dynamic_update_slice x12 -> x0, local copies, waits for them, and re-layouts: 86.4 us -> none  [the longest x8 85.9 us: group_step(): lax.dynamic_update_slice_in_dim(attended_all, attended, begin_at, 3)]
    dot_general x38 -> x1, matrix products: 43 us -> 0.47 us  [on_device(): jnp.einsum('fji,j,fjk->fik', chosen, jnp.asarray(keep, jnp.float32), chos...]
    gather x16 -> x4, local copies, waits for them, and re-layouts: 29 us -> 4.16 us  [the longest x3 2.37 us: on_device(): jnp.take(flat, jnp.asarray(pairs[:, 0] * comp + pairs[:, 1]), axis=1)]
    unnamed x2 -> x0, waiting for transfers between devices: 18.3 us -> none
    pallas_call x0 -> x4, Pallas kernels: none -> 17.6 us  [the longest x1 13.6 us: on_device(): pl.pallas_call(functools.partial(attention_kernel, heads, alpha, comp), g...]
    dynamic_slice x21 -> x2, local copies, waits for them, and re-layouts: 18.9 us -> 2.75 us  [the longest x1 1.51 us: on_device(): lax.dynamic_slice_in_dim(qk_weight, (heads_all + rank * heads) * alpha, h...]
    unnamed x39 -> x34, local copies, waits for them, and re-layouts: 21.9 us -> 7.79 us
    reshape x10 -> x4, local copies, waits for them, and re-layouts: 14.5 us -> 2.21 us  [the longest x1 1.23 us: on_device(): coef = jnp.broadcast_to(picked.reshape(tiles, per_tile, -1).transpose(0,...]
  transfers between devices with their start and end apart: 11 -> 9, of which waited for: 6 -> 4; matrix products, arithmetic and copies ran while one was open for 8% -> 15% of each run, Pallas kernels for 0% -> 1%
where the time goes in v1:
time: 113 us; the launch traced here: 112 us
  waiting for transfers between devices  41.5 us (37%)
  starting transfers between devices  21.5 us (19%)
  local copies, waits for them, and re-layouts  19.5 us (17%)
  Pallas kernels  17.6 us (16%)
  blocking collectives  8.11 us (7%)
  other arithmetic  2.78 us (2%)
    all_to_all x1, waiting for transfers between devices, on_device(): lax.all_to_all(attended, 'head', split_axis=0, concat_axis=0, tiled=True)  20 us
    all_to_all x1, waiting for transfers between devices, on_device(): lax.all_to_all(packed, 'head', split_axis=0, concat_axis=0, tiled=True)  16.7 us
    pallas_call x1, Pallas kernels, on_device(): pl.pallas_call(functools.partial(attention_kernel, heads, alpha, comp), g...  13.6 us
    all_to_all x1, blocking collectives, on_device(): lax.all_to_all(shared, 'head', split_axis=0, concat_axis=0, tiled=True)  8.11 us
    unnamed x34, local copies, waits for them, and re-layouts  7.79 us
    all_to_all x1, starting transfers between devices, on_device(): lax.all_to_all(packed, 'head', split_axis=0, concat_axis=0, tiled=True)  6.48 us
    all_to_all x1, starting transfers between devices, on_device(): lax.all_to_all(attended, 'head', split_axis=0, concat_axis=0, tiled=True)  3.63 us
    all_to_all x1, starting transfers between devices, on_device(): lax.all_to_all(grads, 'head', split_axis=0, concat_axis=0, tiled=True)  3.5 us
  transfers between devices with their start and end apart: 9, of which 4 were waited for; matrix products, arithmetic and copies ran while one was open for 15% of the time, Pallas kernels for 1%

profile of v1, /device:TPU:0, one launch (start us, length us, event | category | flops | bytes accessed | tf_op | source)
XLA Modules:
  0.0 112.2 jit_solution(11873897856960049901)
XLA Ops:
  0.6 1.1 %copy-done = bf16[25,128,128]{2,1,0:T(8,128)(2,1)S(1)} copy-done((bf16[25,128,128]{2,1,0:T(8,128)(2,1)S(1)}, bf16[25,128,128]{2,1,0:T(8,128)(2,1)}, u32[]{:S(2)}) %copy-start) | copy-done | bytes 819224
  1.8 0.9 copy-done.5
  2.7 1.4 %mix_values.1 = bf16[4,29,32,128]{3,2,1,0:T(8,128)(2,1)} custom-call(bf16[25,128,128]{2,1,0:T(8,128)(2,1)S(1)} %copy-done, bf16[5,128,128]{2,1,0:T(8,128)(2,1)S(1)} %copy-done.5), custom_call_target="tpu_custom_call" | custom-call | flops 104857600 | bytes 1638400 | tf_op jit(solution)/shard_map/mix_values/pallas_call | solution.py:241
  4.1 6.5 %all-to-all-start = ((bf16[4,29,32,128]{3,2,1,0:T(8,128)(2,1)}), bf16[4,29,32,128]{3,2,1,0:T(8,128)(2,1)S(1)}, u32[]{:S(2)}, u32[]{:S(2)}) async-start(bf16[4,29,32,128]{3,2,1,0:T(8,128)(2,1)} %mix_values.1), calls=%async_computation | async-start | bytes 1900544 | tf_op jit(solution)/shard_map/all_to_all | solution.py:250
  11.2 2.6 %collective-permute-start.3 = (f32[3,256]{1,0:T(4,128)}, f32[3,256]{1,0:T(4,128)}, u32[]{:S(2)}, u32[]{:S(2)}) collective-permute-start(f32[3,256]{1,0:T(4,128)} %get-tuple-element.13), channel_id=1, source_target_pairs={{4,0},{8,4},{12,8},{16,12},{20,16},{24,20},{28,24},{0,28},{5,1},{9... | collective-permute-start | bytes 9224 | tf_op jit(solution)/shard_map/ppermute | solution.py:267
  13.8 1.3 %mix_back.1 = bf16[4,25,32,128]{3,2,1,0:T(8,128)(2,1)} custom-call(bf16[25,128,128]{2,1,0:T(8,128)(2,1)S(1)} %copy-done.2, bf16[5,128,128]{2,1,0:T(8,128)(2,1)S(1)} %copy-done.3), custom_call_target="tpu_custom_call" | custom-call | flops 104857600 | bytes 1638400 | tf_op jit(solution)/shard_map/mix_back/pallas_call | solution.py:254
  16.0 1.5 %constant_dynamic-slice_fusion = (bf16[128,256]{1,0:T(8,128)(2,1)S(1)}, bf16[128,256]{1,0:T(8,128)(2,1)}) fusion(bf16[128,2048]{1,0:T(8,128)(2,1)} %param.16, s32[]{:T(128)S(6)} %select_n.55, s32[]{:T(128)S(6)} %select_n.54), kind=kLoop, calls=%fused_computation.26 | loop fusion | bytes 262152 | tf_op jit(solution)/shard_map/dynamic_slice | solution.py:306
  17.5 16.7 %all-to-all-done.own = bf16[4,29,32,128]{3,2,1,0:T(8,128)(2,1)S(1)} async-done(((bf16[4,29,32,128]{3,2,1,0:T(8,128)(2,1)}), bf16[4,29,32,128]{3,2,1,0:T(8,128)(2,1)S(1)}, u32[]{:S(2)}, u32[]{:S(2)}) %all-to-all-start) | async-done | bytes 950304 | tf_op jit(solution)/shard_map/all_to_all | solution.py:250
  34.2 3.5 %all-to-all-start.1 = ((bf16[4,25,32,128]{3,2,1,0:T(8,128)(2,1)}), bf16[4,25,32,128]{3,2,1,0:T(8,128)(2,1)S(1)}, u32[]{:S(2)}, u32[]{:S(2)}) async-start(bf16[4,25,32,128]{3,2,1,0:T(8,128)(2,1)} %mix_back.1), calls=%async_computation.1 | async-start | bytes 1638400 | tf_op jit(solution)/shard_map/all_to_all | solution.py:263
  37.7 1.0 fusion.11
  38.7 2.6 %collective-permute-start.1 = (bf16[2,29,32,128]{3,2,1,0:T(8,128)(2,1)}, bf16[2,29,32,128]{3,2,1,0:T(8,128)(2,1)S(1)}, u32[]{:S(2)}, u32[]{:S(2)}) collective-permute-start(bf16[2,29,32,128]{3,2,1,0:T(8,128)(2,1)} %get-tuple-element.6), channel_id=1, source_target_pairs={{4,0},{8,4},{12,8},{16,12},{20,16},{24,20},{28,24},{0,28},{5,1},{9... | collective-permute-start | bytes 1425416 | tf_op jit(solution)/shard_map/ppermute | solution.py:252
  41.4 1.8 %copy.26 = f32[64,25,25]{2,1,0:T(8,128)} copy(f32[64,25,25]{0,2,1:T(8,128)S(1)} %copy-done.9) | data formatting | bytes 320000 | tf_op args[6]
  43.2 1.8 %gather_fusion = f32[8,25,25]{2,1,0:T(8,128)S(1)} fusion(f32[64,25,25]{2,1,0:T(8,128)} %copy.26, s32[1024]{0:T(1024)S(1)} %pad_clamp_fusion.1), kind=kCustom, calls=%fused_computation | custom fusion | bytes 40032 | tf_op jit(solution)/shard_map/jit(_take)/gather | solution.py:272
  46.5 0.7 reshape.78.mask
  47.5 1.4 %gather_fusion.1 = f32[165,8]{1,0:T(8,128)} fusion(f32[8,625]{0,1:T(8,128)S(1)} %copy.28, s32[1024]{0:T(1024)} %pad_clamp_fusion), kind=kCustom, calls=%fused_computation.1 | custom fusion | bytes 11220 | tf_op jit(solution)/shard_map/jit(_take)/gather | solution.py:285
  48.9 0.9 copy.29
  49.9 0.9 broadcast_in_dim.57
  50.8 1.2 %copy.31.coef = f32[4,165,128]{2,1,0:T(8,128)S(1)} copy(f32[4,165,128]{1,2,0:T(8,128)} %bitcast.11) | data formatting | bytes 675840 | tf_op jit(solution)/shard_map/reshape | solution.py:289
  52.0 1.2 %dynamic_slice.9.penalty = f32[4]{0:T(128)} dynamic-slice(f32[16]{0:T(128)} %param.15, s32[]{:T(128)S(6)} %select_n.53), dynamic_slice_sizes={4} | dynamic-slice | bytes 36 | tf_op jit(solution)/shard_map/dynamic_slice | solution.py:309
  53.3 1.3 %maximum_bitcast_fusion.points = f32[8,3,128]{2,1,0:T(4,128)} fusion(f32[3,256]{1,0:T(4,128)} %collective-permute-done.3, f32[3,512]{1,0:T(4,128)} %param.14, f32[3,256]{1,0:T(4,128)} %collective-permute-done.2), kind=kLoop, calls=%fused_computation.11 | loop fusion | flops 6144 | bytes 24576 | tf_op jit(solution)/shard_map/transpose | solution.py:269
  54.6 3.5 %all-to-all-done.1.back = bf16[4,25,32,128]{3,2,1,0:T(8,128)(2,1)S(1)} async-done(((bf16[4,25,32,128]{3,2,1,0:T(8,128)(2,1)}), bf16[4,25,32,128]{3,2,1,0:T(8,128)(2,1)S(1)}, u32[]{:S(2)}, u32[]{:S(2)}) %all-to-all-start.1) | async-done | bytes 819232 | tf_op jit(solution)/shard_map/all_to_all | solution.py:263
  58.0 0.7 copy-done.8
  58.7 0.8 copy-done.4
  59.5 0.7 copy-done.6
  60.3 0.7 copy-done.7
  61.0 13.6 %attention.1 = (bf16[4,25,32,128]{3,2,1,0:T(8,128)(2,1)}, f32[8,3,128]{2,1,0:T(4,128)S(1)}) custom-call(f32[4]{0:T(128)S(1)} %copy-done.8, bf16[2,29,32,128]{3,2,1,0:T(8,128)(2,1)S(1)} %collective-permute-done.before, bf16[4,29,32,128]{3,2,1,0:T(8,128)(2,1)S(1)} %all-to-all-done.own, bf16[2,29,32,128]{3,2,1,0:T(8,128)(2,1)S(1)} %collective-permute-done.1.after, ...), custom_call_target="tpu_custom_call" | custom-call | tf_op jit(solution)/shard_map/attention/pallas_call | solution.py:311
  74.6 2.6 %collective-permute-start.5 = (f32[2,3,128]{2,1,0:T(4,128)S(1)}, f32[2,3,128]{2,1,0:T(4,128)S(1)}, u32[]{:S(2)}, u32[]{:S(2)}) collective-permute-start(f32[2,3,128]{2,1,0:T(4,128)S(1)} %get-tuple-element.11), channel_id=1, source_target_pairs={{4,0},{8,4},{12,8},{16,12},{20,16},{24,20},{28,24},{0,28},{5,1},{9... | collective-permute-start | bytes 9224 | tf_op jit(solution)/shard_map/ppermute | solution.py:354
  77.2 1.3 %collective-permute-done.4 = f32[2,3,128]{2,1,0:T(4,128)S(1)} collective-permute-done((f32[2,3,128]{2,1,0:T(4,128)S(1)}, f32[2,3,128]{2,1,0:T(4,128)S(1)}, u32[]{:S(2)}, u32[]{:S(2)}) %collective-permute-start.4) | collective-permute-done | bytes 3104 | tf_op jit(solution)/shard_map/ppermute | solution.py:355
  78.6 8.1 %all_to_all.20 = f32[4,3,128]{2,1,0:T(4,128)S(1)} all-to-all(f32[4,3,128]{2,1,0:T(4,128)S(1)} %pad_add_fusion), channel_id=1, replica_groups=mesh['dom'=8,'head'=4] {'head'}, dimensions={0} | all-to-all | bytes 12288 | tf_op jit(solution)/shard_map/all_to_all | solution.py:359
  86.7 3.6 %all-to-all-start.2 = ((bf16[4,25,32,128]{3,2,1,0:T(8,128)(2,1)}), bf16[4,25,32,128]{3,2,1,0:T(8,128)(2,1)S(1)}, u32[]{:S(2)}, u32[]{:S(2)}) async-start(bf16[4,25,32,128]{3,2,1,0:T(8,128)(2,1)} %get-tuple-element.4), calls=%async_computation.2 | async-start | bytes 1638400 | tf_op jit(solution)/shard_map/all_to_all | solution.py:353
  90.9 20.0 %all-to-all-done.2.attended = bf16[4,25,32,128]{3,2,1,0:T(8,128)(2,1)S(1)} async-done(((bf16[4,25,32,128]{3,2,1,0:T(8,128)(2,1)}), bf16[4,25,32,128]{3,2,1,0:T(8,128)(2,1)S(1)}, u32[]{:S(2)}, u32[]{:S(2)}) %all-to-all-start.2) | async-done | bytes 819232 | tf_op jit(solution)/shard_map/all_to_all | solution.py:353
  110.9 1.3 %update.1 = bf16[25,128,128]{2,1,0:T(8,128)(2,1)} custom-call(bf16[25,128,128]{2,1,0:T(8,128)(2,1)S(1)} %copy-done.1, bf16[4,25,32,128]{3,2,1,0:T(8,128)(2,1)S(1)} %all-to-all-done.2.attended, bf16[5,128,128]{2,1,0:T(8,128)(2,1)S(1)} %copy-done.3), custom_call_target="tpu_custom_call" | custom-call | flops 104857600 | bytes 1638400 | tf_op jit(solution)/shard_map/update/pallas_call | solution.py:362
  (53 shorter events, 3.9 us)
Async XLA Ops:
  0.6 1.1 %copy-start = (bf16[25,128,128]{2,1,0:T(8,128)(2,1)S(1)}, bf16[25,128,128]{2,1,0:T(8,128)(2,1)}, u32[]{:S(2)}) copy-start(bf16[25,128,128]{2,1,0:T(8,128)(2,1)} %features.3) | copy-start | bytes 2457604
  1.8 0.9 copy-start.5
  4.1 6.5 %copy-start.10 = (f32[3,512]{1,0:T(4,128)S(1)}, f32[3,512]{1,0:T(4,128)}, u32[]{:S(2)}) copy-start(f32[3,512]{1,0:T(4,128)} %param.14) | copy-start | bytes 18436
  4.1 9.7 %copy-start.2 = (bf16[25,128,128]{2,1,0:T(8,128)(2,1)S(1)}, bf16[25,128,128]{2,1,0:T(8,128)(2,1)}, u32[]{:S(2)}) copy-start(bf16[25,128,128]{2,1,0:T(8,128)(2,1)} %cotangent.1) | copy-start | bytes 2457604
  4.1 9.7 %copy-start.3 = (bf16[5,128,128]{2,1,0:T(8,128)(2,1)S(1)}, bf16[5,128,128]{2,1,0:T(8,128)(2,1)}, u32[]{:S(2)}) copy-start(bf16[5,128,128]{2,1,0:T(8,128)(2,1)} %weight.5) | copy-start | bytes 491524
  4.1 30.1 %all-to-all-start = ((bf16[4,29,32,128]{3,2,1,0:T(8,128)(2,1)}), bf16[4,29,32,128]{3,2,1,0:T(8,128)(2,1)S(1)}, u32[]{:S(2)}, u32[]{:S(2)}) async-start(bf16[4,29,32,128]{3,2,1,0:T(8,128)(2,1)} %mix_values.1), calls=%async_computation | async-start | bytes 1900544 | tf_op jit(solution)/shard_map/all_to_all | solution.py:250
  11.2 42.1 %collective-permute-start.2 = (f32[3,256]{1,0:T(4,128)}, f32[3,256]{1,0:T(4,128)}, u32[]{:S(2)}, u32[]{:S(2)}) collective-permute-start(f32[3,256]{1,0:T(4,128)} %get-tuple-element.12), channel_id=1, source_target_pairs={{0,4},{4,8},{8,12},{12,16},{16,20},{20,24},{24,28},{28,0},{1,5},{5... | collective-permute-start | bytes 9224 | tf_op jit(solution)/shard_map/ppermute | solution.py:266
  11.2 42.1 %collective-permute-start.3 = (f32[3,256]{1,0:T(4,128)}, f32[3,256]{1,0:T(4,128)}, u32[]{:S(2)}, u32[]{:S(2)}) collective-permute-start(f32[3,256]{1,0:T(4,128)} %get-tuple-element.13), channel_id=1, source_target_pairs={{4,0},{8,4},{12,8},{16,12},{20,16},{24,20},{28,24},{0,28},{5,1},{9... | collective-permute-start | bytes 9224 | tf_op jit(solution)/shard_map/ppermute | solution.py:267
  13.8 1.3 %copy-start.15 = (s32[8]{0:T(128)S(1)}, s32[8]{0:T(128)}, u32[]{:S(2)}) copy-start(s32[8]{0:T(128)} %param.20) | copy-start | bytes 100
  13.8 1.3 %copy-start.14 = (s32[8]{0:T(128)S(1)}, s32[8]{0:T(128)}, u32[]{:S(2)}) copy-start(s32[8]{0:T(128)} %param.22) | copy-start | bytes 100
  15.1 0.7 copy-start.11
  34.2 23.8 %all-to-all-start.1 = ((bf16[4,25,32,128]{3,2,1,0:T(8,128)(2,1)}), bf16[4,25,32,128]{3,2,1,0:T(8,128)(2,1)S(1)}, u32[]{:S(2)}, u32[]{:S(2)}) async-start(bf16[4,25,32,128]{3,2,1,0:T(8,128)(2,1)} %mix_back.1), calls=%async_computation.1 | async-start | bytes 1638400 | tf_op jit(solution)/shard_map/all_to_all | solution.py:263
  37.7 3.7 %copy-start.9 = (f32[64,25,25]{0,2,1:T(8,128)S(1)}, f32[64,25,25]{0,2,1:T(8,128)}, u32[]{:S(2)}) copy-start(f32[64,25,25]{0,2,1:T(8,128)} %param.19) | copy-start | bytes 480004
  38.7 19.3 %collective-permute-start = (bf16[2,29,32,128]{3,2,1,0:T(8,128)(2,1)}, bf16[2,29,32,128]{3,2,1,0:T(8,128)(2,1)S(1)}, u32[]{:S(2)}, u32[]{:S(2)}) collective-permute-start(bf16[2,29,32,128]{3,2,1,0:T(8,128)(2,1)} %get-tuple-element.7), channel_id=1, source_target_pairs={{0,4},{4,8},{8,12},{12,16},{16,20},{20,24},{24,28},{28,0},{1,5},{5... | collective-permute-start | bytes 1425416 | tf_op jit(solution)/shard_map/ppermute | solution.py:251
  38.7 19.3 %collective-permute-start.1 = (bf16[2,29,32,128]{3,2,1,0:T(8,128)(2,1)}, bf16[2,29,32,128]{3,2,1,0:T(8,128)(2,1)S(1)}, u32[]{:S(2)}, u32[]{:S(2)}) collective-permute-start(bf16[2,29,32,128]{3,2,1,0:T(8,128)(2,1)} %get-tuple-element.6), channel_id=1, source_target_pairs={{4,0},{8,4},{12,8},{16,12},{20,16},{24,20},{28,24},{0,28},{5,1},{9... | collective-permute-start | bytes 1425416 | tf_op jit(solution)/shard_map/ppermute | solution.py:252
  43.2 1.8 %copy-start.13 = (f32[25]{0:T(128)S(1)}, f32[25]{0:T(128)}, u32[]{:S(2)}) copy-start(f32[25]{0:T(128)} %constant.92.clone) | copy-start | bytes 304
  45.0 0.7 copy-start.12
  58.0 0.7 copy-start.8
  58.7 0.8 copy-start.4
  59.5 0.7 copy-start.6
  60.3 0.7 copy-start.7
  74.6 3.9 %collective-permute-start.4 = (f32[2,3,128]{2,1,0:T(4,128)S(1)}, f32[2,3,128]{2,1,0:T(4,128)S(1)}, u32[]{:S(2)}, u32[]{:S(2)}) collective-permute-start(f32[2,3,128]{2,1,0:T(4,128)S(1)} %get-tuple-element.10), channel_id=1, source_target_pairs={{0,4},{4,8},{8,12},{12,16},{16,20},{20,24},{24,28},{28,0},{1,5},{5... | collective-permute-start | bytes 9224 | tf_op jit(solution)/shard_map/ppermute | solution.py:355
  74.6 4.0 %collective-permute-start.5 = (f32[2,3,128]{2,1,0:T(4,128)S(1)}, f32[2,3,128]{2,1,0:T(4,128)S(1)}, u32[]{:S(2)}, u32[]{:S(2)}) collective-permute-start(f32[2,3,128]{2,1,0:T(4,128)S(1)} %get-tuple-element.11), channel_id=1, source_target_pairs={{4,0},{8,4},{12,8},{16,12},{20,16},{24,20},{28,24},{0,28},{5,1},{9... | collective-permute-start | bytes 9224 | tf_op jit(solution)/shard_map/ppermute | solution.py:354
  86.7 24.2 %copy-start.1 = (bf16[25,128,128]{2,1,0:T(8,128)(2,1)S(1)}, bf16[25,128,128]{2,1,0:T(8,128)(2,1)}, u32[]{:S(2)}) copy-start(bf16[25,128,128]{2,1,0:T(8,128)(2,1)} %features.3) | copy-start | bytes 2457604
  86.7 24.2 %all-to-all-start.2 = ((bf16[4,25,32,128]{3,2,1,0:T(8,128)(2,1)}), bf16[4,25,32,128]{3,2,1,0:T(8,128)(2,1)S(1)}, u32[]{:S(2)}, u32[]{:S(2)}) async-start(bf16[4,25,32,128]{3,2,1,0:T(8,128)(2,1)} %get-tuple-element.4), calls=%async_computation.2 | async-start | bytes 1638400 | tf_op jit(solution)/shard_map/all_to_all | solution.py:353

commit v2 on v1

--- a/solution.py
+++ b/solution.py
@@ -65,7 +65,22 @@
         out[k] = (features[k].astype(jnp.float32) + mixed).astype(jnp.bfloat16)
 
 
-def attention_kernel(
+def rotated_rows(coef, comp, source, k, turned):
+    index_of = {pair: n for n, pair in enumerate(pair_table(comp))}
+    l = degree_of(k)
+    total = None
+    for m in range(l * l, (l + 1) * (l + 1)):
+        row = index_of[(m, k) if turned else (k, m)]
+        term = coef[0, row : row + 1, :] * source(m)
+        total = term if total is None else total + term
+    return total
+
+
+def windowed(step, window, get):
+    return jnp.concatenate([get(step + w) for w in range(window)], axis=-1)
+
+
+def gather_kernel(
     heads,
     alpha,
     comp,
@@ -73,7 +88,6 @@
     before,
     own,
     after,
-    back,
     q_weight,
     k_weight,
     coef,
@@ -81,11 +95,10 @@
     points,
     points_t,
     attended,
-    forces,
+    attention_out,
     values_s,
     keys_s,
     queries_s,
-    rotated_s,
     aggregate_s,
 ):
     step = pl.program_id(0)
@@ -106,14 +119,12 @@
         if with_query:
             turned = scalars.T.astype(jnp.bfloat16)
             for h in range(heads):
-                queries_s[at, h] = dot(turned, q_weight[:, h * alpha : (h + 1) * alpha], 1, 0).astype(
-                    jnp.bfloat16
-                )
+                queries_s[at, h] = dot(
+                    turned, q_weight[:, h * alpha : (h + 1) * alpha], 1, 0
+                ).astype(jnp.bfloat16)
 
     @pl.when(step == 0)
     def _():
-        forces[...] = jnp.zeros_like(forces)
-
         def edge(i, carry):
             prepare(before, i, i, False)
             prepare(after, i, i + halo + tiles, False)
@@ -126,70 +137,84 @@
         lax.fori_loop(0, halo, edge, 0)
         lax.fori_loop(0, tiles, inner, 0)
 
-    pairs = pair_table(comp)
-    index_of = {pair: n for n, pair in enumerate(pairs)}
-
-    def rotate(source, k, turned):
-        l = degree_of(k)
-        total = None
-        for m in range(l * l, (l + 1) * (l + 1)):
-            row = index_of[(m, k) if turned else (k, m)]
-            term = coef[0, row : row + 1, :] * source(m)
-            total = term if total is None else total + term
-        return total
-
-    for k in range(comp):
-        rotated_s[k] = (
-            rotate(lambda m: back[step, m].astype(jnp.float32), k, True)
-            .astype(jnp.bfloat16)
-            .astype(jnp.float32)
-        )
-
-    def windowed(get):
-        return jnp.concatenate([get(step + w) for w in range(window)], axis=-1)
-
-    rows = [windowed(lambda s, c=c: points[s, c : c + 1, :]) for c in range(3)]
-    columns = [points_t[step, :, c : c + 1] for c in range(3)]
     distance = None
     for c in range(3):
-        apart = columns[c] - rows[c]
+        row = windowed(step, window, lambda s: points[s, c : c + 1, :])
+        apart = points_t[step, :, c : c + 1] - row
         distance = apart * apart if distance is None else distance + apart * apart
-    per_tile = atoms // BLOCK
     hidden = jnp.concatenate(
         [
             jnp.broadcast_to(mask[0, r : r + 1, :], (BLOCK, window * atoms))
-            for r in range(per_tile)
+            for r in range(atoms // BLOCK)
         ],
         axis=0,
     )
     distance = jnp.maximum(distance, hidden)
-    total = jnp.zeros((atoms, window * atoms), jnp.float32)
     scale = 1.0 / math.sqrt(alpha)
     for h in range(heads):
-        strength = penalty[h]
-        keys = windowed(lambda s: keys_s[s, h])
-        values = windowed(lambda s: values_s[s, h])
-        logits = dot(queries_s[step, h], keys, 1, 0) * scale - strength * distance
+        keys = windowed(step, window, lambda s: keys_s[s, h])
+        values = windowed(step, window, lambda s: values_s[s, h])
+        logits = dot(queries_s[step, h], keys, 1, 0) * scale - penalty[h] * distance
         peaks = jnp.max(logits, axis=1, keepdims=True)
         exponent = jnp.exp(logits - peaks)
         inverse = 1.0 / jnp.sum(exponent, axis=1, keepdims=True)
         attention = exponent * inverse
+        attention_out[0, h] = attention
         aggregate = dot(values, attention.astype(jnp.bfloat16), 1, 1)
         aggregate_s[:, h * head_width : (h + 1) * head_width] = aggregate.reshape(
             comp, head_width, atoms
         )
-        turned = rotated_s[:, h * head_width : (h + 1) * head_width].reshape(comp * head_width, atoms)
+    for k in range(comp):
+        attended[0, k] = rotated_rows(coef, comp, lambda m: aggregate_s[m], k, False).astype(
+            jnp.bfloat16
+        )
+
+
+def force_kernel(
+    heads,
+    penalty,
+    back,
+    attention_in,
+    values_s,
+    coef,
+    points,
+    points_t,
+    forces,
+    rotated_s,
+):
+    step = pl.program_id(0)
+    _, comp, width, atoms = back.shape
+    head_width = width // heads
+    window = attention_in.shape[3] // atoms
+    halo = window // 2
+
+    @pl.when(step == 0)
+    def _():
+        forces[...] = jnp.zeros_like(forces)
+
+    for k in range(comp):
+        rotated_s[k] = (
+            rotated_rows(coef, comp, lambda m: back[0, m].astype(jnp.float32), k, True)
+            .astype(jnp.bfloat16)
+            .astype(jnp.float32)
+        )
+    total = jnp.zeros((atoms, window * atoms), jnp.float32)
+    for h in range(heads):
+        values = windowed(step, window, lambda s: values_s[s, h])
+        attention = attention_in[0, h]
+        turned = rotated_s[:, h * head_width : (h + 1) * head_width].reshape(
+            comp * head_width, atoms
+        )
         weight_grads = dot(turned.T.astype(jnp.bfloat16), values, 1, 0)
         mean = jnp.sum(attention * weight_grads, axis=1, keepdims=True)
-        total = total + (2.0 * strength) * (attention * (weight_grads - mean))
-    for k in range(comp):
-        attended[0, k] = rotate(lambda m: aggregate_s[m], k, False).astype(jnp.bfloat16)
+        total = total + (2.0 * penalty[h]) * (attention * (weight_grads - mean))
 
     lane = lax.broadcasted_iota(jnp.int32, (atoms, atoms), 1)
     mine = jnp.zeros((atoms, atoms), jnp.float32)
     theirs = []
     for c in range(3):
-        weighted = total * (columns[c] - rows[c])
+        row = windowed(step, window, lambda s: points[s, c : c + 1, :])
+        weighted = total * (points_t[step, :, c : c + 1] - row)
         mine = jnp.where(lane == c, jnp.sum(weighted, axis=1, keepdims=True), mine)
         theirs.append(jnp.sum(weighted, axis=0, keepdims=True))
     mine = mine.T
@@ -308,40 +333,46 @@
     )
     penalty_here = lax.dynamic_slice_in_dim(penalty, rank * heads, heads)
 
-    attended, forces = pl.pallas_call(
-        functools.partial(attention_kernel, heads, alpha, comp),
+    smem = pl.BlockSpec(memory_space=pltpu.SMEM)
+    coef_spec = pl.BlockSpec((1, len(pairs), atoms), lambda t: (t, 0, 0))
+    tile_spec = pl.BlockSpec((1, comp, width, atoms), lambda t: (t, 0, 0, 0))
+    weight_shape = (tiles, heads, atoms, window * atoms)
+    weight_spec = pl.BlockSpec((1,) + weight_shape[1:], lambda t: (t, 0, 0, 0))
+    half_cost = pl.CostEstimate(
+        flops=4 * tiles * heads * comp * head_width * atoms * window * atoms,
+        bytes_accessed=16 * 2**20,
+        transcendentals=math.prod(weight_shape),
+    )
+    attended, attention, head_values = pl.pallas_call(
+        functools.partial(gather_kernel, heads, alpha, comp),
         grid=(tiles,),
         out_shape=(
             jax.ShapeDtypeStruct((tiles, comp, width, atoms), jnp.bfloat16),
-            jax.ShapeDtypeStruct((slots, 3, atoms), jnp.float32),
+            jax.ShapeDtypeStruct(weight_shape, jnp.float32),
+            jax.ShapeDtypeStruct((slots, heads, comp * head_width, atoms), jnp.bfloat16),
         ),
-        in_specs=[pl.BlockSpec(memory_space=pltpu.SMEM)]
-        + [vmem()] * 6
+        in_specs=[smem]
+        + [vmem()] * 5
         + [
-            pl.BlockSpec((1, len(pairs), atoms), lambda t: (t, 0, 0)),
+            coef_spec,
             pl.BlockSpec((1, per_tile, window * atoms), lambda t: (t, 0, 0)),
             vmem(),
             vmem(),
         ],
-        out_specs=(
-            pl.BlockSpec((1, comp, width, atoms), lambda t: (t, 0, 0, 0)),
-            vmem(),
-        ),
+        out_specs=(tile_spec, weight_spec, vmem()),
         scratch_shapes=[
-            pltpu.VMEM((slots, heads, comp * head_width, atoms), jnp.bfloat16),
             pltpu.VMEM((slots, heads, alpha, atoms), jnp.bfloat16),
             pltpu.VMEM((tiles, heads, atoms, alpha), jnp.bfloat16),
             pltpu.VMEM((comp, width, atoms), jnp.float32),
-            pltpu.VMEM((comp, width, atoms), jnp.float32),
         ],
         compiler_params=params,
-        name="attention",
+        cost_estimate=half_cost,
+        name="aggregate",
     )(
         penalty_here,
         before,
         own,
         after,
-        back,
         q_weight,
         k_weight,
         coef,
@@ -349,6 +380,17 @@
         points,
         points_t,
     )
+    forces = pl.pallas_call(
+        functools.partial(force_kernel, heads),
+        grid=(tiles,),
+        out_shape=jax.ShapeDtypeStruct((slots, 3, atoms), jnp.float32),
+        in_specs=[smem, tile_spec, weight_spec, vmem(), coef_spec, vmem(), vmem()],
+        out_specs=vmem(),
+        scratch_shapes=[pltpu.VMEM((comp, width, atoms), jnp.float32)],
+        compiler_params=params,
+        cost_estimate=half_cost,
+        name="force_terms",
+    )(penalty_here, back, attention, head_values, coef, points, points_t)
 
     arrived = lax.all_to_all(attended, "head", split_axis=0, concat_axis=0, tiled=True)
     low = lax.ppermute(forces[:halo], "dom", down)
@@ -356,8 +398,12 @@
     shared = forces[halo : halo + tiles]
     shared = shared + jnp.concatenate([high, jnp.zeros_like(shared[halo:])], axis=0)
     shared = shared + jnp.concatenate([jnp.zeros_like(shared[halo:]), low], axis=0)
-    shares = lax.all_to_all(shared, "head", split_axis=0, concat_axis=0, tiled=True)
-    force = jnp.sum(shares, axis=0)
+    force = lax.dynamic_index_in_dim(shared, rank, 0, keepdims=False)
+    for shift in range(1, ranks):
+        share = lax.dynamic_index_in_dim(shared, (rank + shift) % ranks, 0, keepdims=False)
+        force = force + lax.ppermute(
+            share, "head", [(i, (i + shift) % ranks) for i in range(ranks)]
+        )
 
     updated = pl.pallas_call(
         update_kernel,

time: 113 us -> 95.7 us (0.85)
  waiting for transfers between devices: 41.5 us -> 22.8 us
  blocking collectives: 8.11 us -> 0 us
  starting transfers between devices: 21.5 us -> 29 us
  local copies, waits for them, and re-layouts: 19.5 us -> 22.1 us
  other arithmetic: 2.78 us -> 0.88 us
    all_to_all x1, waiting for transfers between devices: 20 us -> 0.01 us  [on_device(): lax.all_to_all(attended, 'head', split_axis=0, concat_axis=0, tiled=True)]
    all_to_all x1 -> x0, blocking collectives: 8.11 us -> none  [on_device(): lax.all_to_all(shared, 'head', split_axis=0, concat_axis=0, tiled=True)]
    unnamed x34 -> x40, local copies, waits for them, and re-layouts: 7.79 us -> 14.4 us
    ppermute x0 -> x3, starting transfers between devices: none -> 5.88 us  [on_device(): lax.ppermute(share, 'head', [(i, (i + shift) % ranks) for i in range(rank...]
    ppermute x0 -> x3, waiting for transfers between devices: none -> 3.48 us  [on_device(): lax.ppermute(share, 'head', [(i, (i + shift) % ranks) for i in range(rank...]
    all_to_all x1, waiting for transfers between devices: 3.46 us -> 0.01 us  [on_device(): lax.all_to_all(grads, 'head', split_axis=0, concat_axis=0, tiled=True)]
    ppermute x1, waiting for transfers between devices: 0.01 us -> 2.14 us  [on_device(): before = lax.ppermute(own[tiles - halo:], 'dom', up)]
    gather x3, local copies, waits for them, and re-layouts: 2.37 us -> 0.75 us  [on_device(): jnp.take(flat, jnp.asarray(pairs[:, 0] * comp + pairs[:, 1]), axis=1)]
  transfers between devices with their start and end apart: 9 -> 12, of which waited for: 4 -> 4; matrix products, arithmetic and copies ran while one was open for 15% -> 12% of each run, Pallas kernels for 1% -> 17%
where the time goes in v2:
time: 95.7 us; the launch traced here: 94.9 us
  starting transfers between devices  29 us (30%)
  waiting for transfers between devices  22.8 us (24%)
  local copies, waits for them, and re-layouts  22.1 us (23%)
  Pallas kernels  18.7 us (20%)
    all_to_all x1, waiting for transfers between devices, on_device(): lax.all_to_all(packed, 'head', split_axis=0, concat_axis=0, tiled=True)  15.8 us
    unnamed x40, local copies, waits for them, and re-layouts  14.4 us
    pallas_call x1, Pallas kernels, on_device(): pl.pallas_call(functools.partial(gather_kernel, heads, alpha, comp), grid...  10.2 us
    all_to_all x1, starting transfers between devices, on_device(): lax.all_to_all(packed, 'head', split_axis=0, concat_axis=0, tiled=True)  6.48 us
    ppermute x3, starting transfers between devices, on_device(): lax.ppermute(share, 'head', [(i, (i + shift) % ranks) for i in range(rank...  5.88 us
    all_to_all x1, starting transfers between devices, on_device(): lax.all_to_all(attended, 'head', split_axis=0, concat_axis=0, tiled=True)  5.19 us
    pallas_call x1, Pallas kernels, on_device(): pl.pallas_call(functools.partial(force_kernel, heads), grid=(tiles,), out...  4.55 us
    all_to_all x1, starting transfers between devices, on_device(): lax.all_to_all(grads, 'head', split_axis=0, concat_axis=0, tiled=True)  3.5 us
  transfers between devices with their start and end apart: 12, of which 4 were waited for; matrix products, arithmetic and copies ran while one was open for 12% of the time, Pallas kernels for 17%

profile of v2, /device:TPU:0, one launch (start us, length us, event | category | flops | bytes accessed | tf_op | source)
XLA Modules:
  0.0 94.9 jit_solution(15178896310525050380)
XLA Ops:
  0.7 1.1 %copy-done.2 = bf16[25,128,128]{2,1,0:T(8,128)(2,1)S(1)} copy-done((bf16[25,128,128]{2,1,0:T(8,128)(2,1)S(1)}, bf16[25,128,128]{2,1,0:T(8,128)(2,1)}, u32[]{:S(2)}) %copy-start.2) | copy-done | bytes 819224
  1.8 0.9 copy-done.10
  2.7 1.4 %mix_values.1 = bf16[4,29,32,128]{3,2,1,0:T(8,128)(2,1)} custom-call(bf16[25,128,128]{2,1,0:T(8,128)(2,1)S(1)} %copy-done.2, bf16[5,128,128]{2,1,0:T(8,128)(2,1)S(1)} %copy-done.10), custom_call_target="tpu_custom_call" | custom-call | flops 104857600 | bytes 1638400 | tf_op jit(solution)/shard_map/mix_values/pallas_call | solution.py:266
  4.1 6.5 %all-to-all-start = ((bf16[4,29,32,128]{3,2,1,0:T(8,128)(2,1)}), bf16[4,29,32,128]{3,2,1,0:T(8,128)(2,1)S(1)}, u32[]{:S(2)}, u32[]{:S(2)}) async-start(bf16[4,29,32,128]{3,2,1,0:T(8,128)(2,1)} %mix_values.1), calls=%async_computation | async-start | bytes 1900544 | tf_op jit(solution)/shard_map/all_to_all | solution.py:275
  11.3 2.6 %collective-permute-start.3 = (f32[3,256]{1,0:T(4,128)S(1)}, f32[3,256]{1,0:T(4,128)S(1)}, u32[]{:S(2)}, u32[]{:S(2)}) collective-permute-start(f32[3,256]{1,0:T(4,128)S(1)} %get-tuple-element.18), channel_id=1, source_target_pairs={{4,0},{8,4},{12,8},{16,12},{20,16},{24,20},{28,24},{0,28},{5,1},{9... | collective-permute-start | bytes 9224 | tf_op jit(solution)/shard_map/ppermute | solution.py:292
  13.9 1.1 %copy-done.6 = bf16[25,128,128]{2,1,0:T(8,128)(2,1)S(1)} copy-done((bf16[25,128,128]{2,1,0:T(8,128)(2,1)S(1)}, bf16[25,128,128]{2,1,0:T(8,128)(2,1)}, u32[]{:S(2)}) %copy-start.6) | copy-done | bytes 819224
  15.1 0.9 copy-done.8
  16.0 1.3 %mix_back.1 = bf16[4,25,32,128]{3,2,1,0:T(8,128)(2,1)} custom-call(bf16[25,128,128]{2,1,0:T(8,128)(2,1)S(1)} %copy-done.6, bf16[5,128,128]{2,1,0:T(8,128)(2,1)S(1)} %copy-done.8), custom_call_target="tpu_custom_call" | custom-call | flops 104857600 | bytes 1638400 | tf_op jit(solution)/shard_map/mix_back/pallas_call | solution.py:279
  18.4 15.8 %all-to-all-done.own = bf16[4,29,32,128]{3,2,1,0:T(8,128)(2,1)S(1)} async-done(((bf16[4,29,32,128]{3,2,1,0:T(8,128)(2,1)}), bf16[4,29,32,128]{3,2,1,0:T(8,128)(2,1)S(1)}, u32[]{:S(2)}, u32[]{:S(2)}) %all-to-all-start) | async-done | bytes 950304 | tf_op jit(solution)/shard_map/all_to_all | solution.py:275
  34.2 3.5 %all-to-all-start.2 = ((bf16[4,25,32,128]{3,2,1,0:T(8,128)(2,1)}), bf16[4,25,32,128]{3,2,1,0:T(8,128)(2,1)S(1)}, u32[]{:S(2)}, u32[]{:S(2)}) async-start(bf16[4,25,32,128]{3,2,1,0:T(8,128)(2,1)} %mix_back.1), calls=%async_computation.2 | async-start | bytes 1638400 | tf_op jit(solution)/shard_map/all_to_all | solution.py:288
  37.8 1.0 %fusion.14 = (bf16[2,29,32,128]{3,2,1,0:T(8,128)(2,1)}, bf16[2,29,32,128]{3,2,1,0:T(8,128)(2,1)}) fusion(bf16[4,29,32,128]{3,2,1,0:T(8,128)(2,1)S(1)} %all-to-all-done.own), kind=kLoop, calls=%fused_computation.36 | loop fusion | bytes 1900544 | tf_op jit(solution)/shard_map/slice | solution.py:277
  38.8 2.6 %collective-permute-start.1 = (bf16[2,29,32,128]{3,2,1,0:T(8,128)(2,1)}, bf16[2,29,32,128]{3,2,1,0:T(8,128)(2,1)}, u32[]{:S(2)}, u32[]{:S(2)}) collective-permute-start(bf16[2,29,32,128]{3,2,1,0:T(8,128)(2,1)} %get-tuple-element.8), channel_id=1, source_target_pairs={{4,0},{8,4},{12,8},{16,12},{20,16},{24,20},{28,24},{0,28},{5,1},{9... | collective-permute-start | bytes 1425416 | tf_op jit(solution)/shard_map/ppermute | solution.py:277
  41.5 1.8 %copy.27 = f32[64,25,25]{2,1,0:T(8,128)} copy(f32[64,25,25]{0,2,1:T(8,128)S(1)} %copy-done.11) | data formatting | bytes 320000 | tf_op args[6]
  43.3 1.8 %gather_fusion = f32[8,25,25]{2,1,0:T(8,128)S(1)} fusion(f32[64,25,25]{2,1,0:T(8,128)} %copy.27, s32[1024]{0:T(1024)S(1)} %pad_clamp_fusion.1), kind=kCustom, calls=%fused_computation | custom fusion | bytes 40032 | tf_op jit(solution)/shard_map/jit(_take)/gather | solution.py:297
  47.6 1.2 %copy.32.coef = f32[4,165,128]{2,1,0:T(8,128)S(1)} copy(f32[4,165,128]{1,2,0:T(8,128)} %bitcast.24) | data formatting | bytes 675840 | tf_op jit(solution)/shard_map/reshape | solution.py:314
  49.1 2.1 %collective-permute-done.before = bf16[2,29,32,128]{3,2,1,0:T(8,128)(2,1)S(1)} collective-permute-done((bf16[2,29,32,128]{3,2,1,0:T(8,128)(2,1)}, bf16[2,29,32,128]{3,2,1,0:T(8,128)(2,1)S(1)}, u32[]{:S(2)}, u32[]{:S(2)}) %collective-permute-start) | collective-permute-done | bytes 475168 | tf_op jit(solution)/shard_map/ppermute | solution.py:276
  51.3 10.2 %aggregate.1 = (bf16[4,25,32,128]{3,2,1,0:T(8,128)(2,1)S(1)}, f32[4,4,128,640]{3,2,1,0:T(8,128)S(1)}, bf16[8,4,200,128]{3,2,1,0:T(8,128)(2,1)S(1)}) custom-call(f32[4]{0:T(128)S(1)} %dynamic_slice.22.penalty, bf16[2,29,32,128]{3,2,1,0:T(8,128)(2,1)S(1)} %collective-permute-done.before, bf16[4,29,32,128]{3,2,1,0:T(8,128)(2,1)S(1)} %all-to-all-done.own, ...), custom_call_target="tpu_custom_call" | custom-call | flops 1048576000 | bytes 16777216 | tf_op jit(solution)/shard_map/aggregate/pallas_call | solution.py:346
  61.6 2.3 %copy-done = f32[4,4,128,640]{3,2,1,0:T(8,128)} copy-done((f32[4,4,128,640]{3,2,1,0:T(8,128)}, f32[4,4,128,640]{3,2,1,0:T(8,128)S(1)}, u32[]{:S(2)}) %copy-start) | copy-done | bytes 5242904
  63.9 1.2 %copy-done.4 = bf16[8,4,200,128]{3,2,1,0:T(8,128)(2,1)} copy-done((bf16[8,4,200,128]{3,2,1,0:T(8,128)(2,1)}, bf16[8,4,200,128]{3,2,1,0:T(8,128)(2,1)S(1)}, u32[]{:S(2)}) %copy-start.4) | copy-done | bytes 1638424
  65.1 0.9 copy-done.7
  66.0 5.2 %all-to-all-start.1 = ((bf16[4,25,32,128]{3,2,1,0:T(8,128)(2,1)}), bf16[4,25,32,128]{3,2,1,0:T(8,128)(2,1)S(1)}, u32[]{:S(2)}, u32[]{:S(2)}) async-start(bf16[4,25,32,128]{3,2,1,0:T(8,128)(2,1)} %copy-done.7), calls=%async_computation.1 | async-start | bytes 1638400 | tf_op jit(solution)/shard_map/all_to_all | solution.py:395
  71.2 2.5 %copy-done.1 = f32[4,4,128,640]{3,2,1,0:T(8,128)S(1)} copy-done((f32[4,4,128,640]{3,2,1,0:T(8,128)S(1)}, f32[4,4,128,640]{3,2,1,0:T(8,128)}, u32[]{:S(2)}) %copy-start.1) | copy-done | bytes 5242904
  73.7 1.4 %copy-done.5 = bf16[8,4,200,128]{3,2,1,0:T(8,128)(2,1)S(1)} copy-done((bf16[8,4,200,128]{3,2,1,0:T(8,128)(2,1)S(1)}, bf16[8,4,200,128]{3,2,1,0:T(8,128)(2,1)}, u32[]{:S(2)}) %copy-start.5) | copy-done | bytes 1638424
  75.1 4.5 %force_terms.1 = f32[8,3,128]{2,1,0:T(4,128)S(1)} custom-call(f32[4]{0:T(128)S(1)} %dynamic_slice.22.penalty, bf16[4,25,32,128]{3,2,1,0:T(8,128)(2,1)S(1)} %all-to-all-done.2.back, f32[4,4,128,640]{3,2,1,0:T(8,128)S(1)} %copy-done.1, bf16[8,4,200,128]{3,2,1,0:T(8,128)(2,1)S(1)} %copy-done.5, f32[4,165,128]{2,1,0:T(8,128)S(1)} %copy.32.coef, ...), custom_call_target="tpu_custom_call" | custom-call | flops 1048576000 | bytes 16777216 | tf_op jit(solution)/shard_map/force_terms/pallas_call | solution.py:383
  79.6 1.5 %collective-permute-start.4 = (f32[2,3,128]{2,1,0:T(4,128)S(1)}, f32[2,3,128]{2,1,0:T(4,128)S(1)}, u32[]{:S(2)}, u32[]{:S(2)}) collective-permute-start(f32[2,3,128]{2,1,0:T(4,128)S(1)} %get-tuple-element.12), channel_id=1, source_target_pairs={{0,4},{4,8},{8,12},{12,16},{16,20},{20,24},{24,28},{28,0},{1,5},{5... | collective-permute-start | bytes 9224 | tf_op jit(solution)/shard_map/ppermute | solution.py:397
  81.2 1.2 %collective-permute-start.5 = (f32[2,3,128]{2,1,0:T(4,128)S(1)}, f32[2,3,128]{2,1,0:T(4,128)S(1)}, u32[]{:S(2)}, u32[]{:S(2)}) collective-permute-start(f32[2,3,128]{2,1,0:T(4,128)S(1)} %get-tuple-element.13), channel_id=1, source_target_pairs={{4,0},{8,4},{12,8},{16,12},{20,16},{24,20},{28,24},{0,28},{5,1},{9... | collective-permute-start | bytes 9224 | tf_op jit(solution)/shard_map/ppermute | solution.py:396
  82.3 1.3 %collective-permute-done.4 = f32[2,3,128]{2,1,0:T(4,128)S(1)} collective-permute-done((f32[2,3,128]{2,1,0:T(4,128)S(1)}, f32[2,3,128]{2,1,0:T(4,128)S(1)}, u32[]{:S(2)}, u32[]{:S(2)}) %collective-permute-start.4) | collective-permute-done | bytes 3104 | tf_op jit(solution)/shard_map/ppermute | solution.py:397
  83.7 2.1 %collective-permute-start.6 = (f32[3,128]{1,0:T(4,128)S(1)}, f32[3,128]{1,0:T(4,128)S(1)}, u32[]{:S(2)}, u32[]{:S(2)}) collective-permute-start(f32[3,128]{1,0:T(4,128)S(1)} %get-tuple-element.14), channel_id=1, source_target_pairs={{0,1},{1,2},{2,3},{3,0},{4,5},{5,6},{6,7},{7,4},{8,9},{9,10},{10,1... | collective-permute-start | bytes 4616 | tf_op jit(solution)/shard_map/ppermute | solution.py:404
  85.7 2.4 %collective-permute-start.7 = (f32[3,128]{1,0:T(4,128)S(1)}, f32[3,128]{1,0:T(4,128)S(1)}, u32[]{:S(2)}, u32[]{:S(2)}) collective-permute-start(f32[3,128]{1,0:T(4,128)S(1)} %get-tuple-element.16), channel_id=1, source_target_pairs={{0,2},{1,3},{2,0},{3,1},{4,6},{5,7},{6,4},{7,5},{8,10},{9,11},{10,... | collective-permute-start | bytes 4616 | tf_op jit(solution)/shard_map/ppermute | solution.py:404
  88.1 1.5 %collective-permute-start.8 = (f32[3,128]{1,0:T(4,128)S(1)}, f32[3,128]{1,0:T(4,128)S(1)}, u32[]{:S(2)}, u32[]{:S(2)}) collective-permute-start(f32[3,128]{1,0:T(4,128)S(1)} %get-tuple-element.15), channel_id=1, source_target_pairs={{0,3},{1,0},{2,1},{3,2},{4,7},{5,4},{6,5},{7,6},{8,11},{9,8},{10,9... | collective-permute-start | bytes 4616 | tf_op jit(solution)/shard_map/ppermute | solution.py:404
  89.6 3.5 %collective-permute-done.7 = f32[3,128]{1,0:T(4,128)S(1)} collective-permute-done((f32[3,128]{1,0:T(4,128)S(1)}, f32[3,128]{1,0:T(4,128)S(1)}, u32[]{:S(2)}, u32[]{:S(2)}) %collective-permute-start.7) | collective-permute-done | bytes 1568 | tf_op jit(solution)/shard_map/ppermute | solution.py:404
  93.6 1.3 %update.1 = bf16[25,128,128]{2,1,0:T(8,128)(2,1)} custom-call(bf16[25,128,128]{2,1,0:T(8,128)(2,1)S(1)} %copy-done.3, bf16[4,25,32,128]{3,2,1,0:T(8,128)(2,1)S(1)} %all-to-all-done.1.attended, bf16[5,128,128]{2,1,0:T(8,128)(2,1)S(1)} %copy-done.9), custom_call_target="tpu_custom_call" | custom-call | flops 104857600 | bytes 1638400 | tf_op jit(solution)/shard_map/update/pallas_call | solution.py:408
  (66 shorter events, 5.4 us)
Async XLA Ops:
  0.6 44.4 %copy-start.15 = (f32[25]{0:T(128)S(1)}, f32[25]{0:T(128)}, u32[]{:S(2)}) copy-start(f32[25]{0:T(128)} %constant.122.clone) | copy-start | bytes 304
  0.6 1.2 %copy-start.2 = (bf16[25,128,128]{2,1,0:T(8,128)(2,1)S(1)}, bf16[25,128,128]{2,1,0:T(8,128)(2,1)}, u32[]{:S(2)}) copy-start(bf16[25,128,128]{2,1,0:T(8,128)(2,1)} %features.3) | copy-start | bytes 2457604
  1.8 0.9 copy-start.10
  2.7 15.5 %copy-start.16 = (s32[8]{0:T(128)S(1)}, s32[8]{0:T(128)}, u32[]{:S(2)}) copy-start(s32[8]{0:T(128)} %param.20) | copy-start | bytes 100
  2.7 15.5 %copy-start.17 = (s32[8]{0:T(128)S(1)}, s32[8]{0:T(128)}, u32[]{:S(2)}) copy-start(s32[8]{0:T(128)} %param.22) | copy-start | bytes 100
  2.7 15.6 %copy-start.13 = (s32[8,8]{1,0:T(8,128)S(1)}, s32[8,8]{1,0:T(8,128)}, u32[]{:S(2)}) copy-start(s32[8,8]{1,0:T(8,128)} %param.21) | copy-start | bytes 772
  2.7 38.8 %copy-start.11 = (f32[64,25,25]{0,2,1:T(8,128)S(1)}, f32[64,25,25]{0,2,1:T(8,128)}, u32[]{:S(2)}) copy-start(f32[64,25,25]{0,2,1:T(8,128)} %param.19) | copy-start | bytes 480004
  4.1 41.5 %copy-start.14 = (s32[165]{0:T(256)S(1)}, s32[165]{0:T(256)}, u32[]{:S(2)}) copy-start(s32[165]{0:T(256)} %constant.136) | copy-start | bytes 1984
  4.1 41.5 %copy-start.12 = (f32[3,512]{1,0:T(4,128)S(1)}, f32[3,512]{1,0:T(4,128)}, u32[]{:S(2)}) copy-start(f32[3,512]{1,0:T(4,128)} %param.14) | copy-start | bytes 18436
  4.1 30.1 %all-to-all-start = ((bf16[4,29,32,128]{3,2,1,0:T(8,128)(2,1)}), bf16[4,29,32,128]{3,2,1,0:T(8,128)(2,1)S(1)}, u32[]{:S(2)}, u32[]{:S(2)}) async-start(bf16[4,29,32,128]{3,2,1,0:T(8,128)(2,1)} %mix_values.1), calls=%async_computation | async-start | bytes 1900544 | tf_op jit(solution)/shard_map/all_to_all | solution.py:275
  10.6 38.4 %copy-start.18 = (f32[16]{0:T(128)S(1)}, f32[16]{0:T(128)}, u32[]{:S(2)}) copy-start(f32[16]{0:T(128)} %param.15) | copy-start | bytes 196
  11.3 37.8 %collective-permute-start.2 = (f32[3,256]{1,0:T(4,128)S(1)}, f32[3,256]{1,0:T(4,128)S(1)}, u32[]{:S(2)}, u32[]{:S(2)}) collective-permute-start(f32[3,256]{1,0:T(4,128)S(1)} %get-tuple-element.17), channel_id=1, source_target_pairs={{0,4},{4,8},{8,12},{12,16},{16,20},{20,24},{24,28},{28,0},{1,5},{5... | collective-permute-start | bytes 9224 | tf_op jit(solution)/shard_map/ppermute | solution.py:291
  11.3 37.8 %collective-permute-start.3 = (f32[3,256]{1,0:T(4,128)S(1)}, f32[3,256]{1,0:T(4,128)S(1)}, u32[]{:S(2)}, u32[]{:S(2)}) collective-permute-start(f32[3,256]{1,0:T(4,128)S(1)} %get-tuple-element.18), channel_id=1, source_target_pairs={{4,0},{8,4},{12,8},{16,12},{20,16},{24,20},{28,24},{0,28},{5,1},{9... | collective-permute-start | bytes 9224 | tf_op jit(solution)/shard_map/ppermute | solution.py:292
  13.9 1.1 %copy-start.6 = (bf16[25,128,128]{2,1,0:T(8,128)(2,1)S(1)}, bf16[25,128,128]{2,1,0:T(8,128)(2,1)}, u32[]{:S(2)}) copy-start(bf16[25,128,128]{2,1,0:T(8,128)(2,1)} %cotangent.1) | copy-start | bytes 2457604
  15.1 0.9 copy-start.8
  34.2 31.8 %all-to-all-start.2 = ((bf16[4,25,32,128]{3,2,1,0:T(8,128)(2,1)}), bf16[4,25,32,128]{3,2,1,0:T(8,128)(2,1)S(1)}, u32[]{:S(2)}, u32[]{:S(2)}) async-start(bf16[4,25,32,128]{3,2,1,0:T(8,128)(2,1)} %mix_back.1), calls=%async_computation.2 | async-start | bytes 1638400 | tf_op jit(solution)/shard_map/all_to_all | solution.py:288
  38.8 12.4 %collective-permute-start = (bf16[2,29,32,128]{3,2,1,0:T(8,128)(2,1)}, bf16[2,29,32,128]{3,2,1,0:T(8,128)(2,1)S(1)}, u32[]{:S(2)}, u32[]{:S(2)}) collective-permute-start(bf16[2,29,32,128]{3,2,1,0:T(8,128)(2,1)} %get-tuple-element.9), channel_id=1, source_target_pairs={{0,4},{4,8},{8,12},{12,16},{16,20},{20,24},{24,28},{28,0},{1,5},{5... | collective-permute-start | bytes 1425416 | tf_op jit(solution)/shard_map/ppermute | solution.py:276
  38.8 12.5 %collective-permute-start.1 = (bf16[2,29,32,128]{3,2,1,0:T(8,128)(2,1)}, bf16[2,29,32,128]{3,2,1,0:T(8,128)(2,1)}, u32[]{:S(2)}, u32[]{:S(2)}) collective-permute-start(bf16[2,29,32,128]{3,2,1,0:T(8,128)(2,1)} %get-tuple-element.8), channel_id=1, source_target_pairs={{4,0},{8,4},{12,8},{16,12},{20,16},{24,20},{28,24},{0,28},{5,1},{9... | collective-permute-start | bytes 1425416 | tf_op jit(solution)/shard_map/ppermute | solution.py:277
  61.6 2.3 %copy-start = (f32[4,4,128,640]{3,2,1,0:T(8,128)}, f32[4,4,128,640]{3,2,1,0:T(8,128)S(1)}, u32[]{:S(2)}) copy-start(f32[4,4,128,640]{3,2,1,0:T(8,128)S(1)} %get-tuple-element.6.attention_in) | copy-start | bytes 15728644
  63.9 1.2 %copy-start.4 = (bf16[8,4,200,128]{3,2,1,0:T(8,128)(2,1)}, bf16[8,4,200,128]{3,2,1,0:T(8,128)(2,1)S(1)}, u32[]{:S(2)}) copy-start(bf16[8,4,200,128]{3,2,1,0:T(8,128)(2,1)S(1)} %get-tuple-element.7.values_s) | copy-start | bytes 4915204
  65.1 0.9 copy-start.7
  66.0 27.7 %copy-start.3 = (bf16[25,128,128]{2,1,0:T(8,128)(2,1)S(1)}, bf16[25,128,128]{2,1,0:T(8,128)(2,1)}, u32[]{:S(2)}) copy-start(bf16[25,128,128]{2,1,0:T(8,128)(2,1)} %features.3) | copy-start | bytes 2457604
  66.0 27.7 %copy-start.9 = (bf16[5,128,128]{2,1,0:T(8,128)(2,1)S(1)}, bf16[5,128,128]{2,1,0:T(8,128)(2,1)}, u32[]{:S(2)}) copy-start(bf16[5,128,128]{2,1,0:T(8,128)(2,1)} %weight.5) | copy-start | bytes 491524
  66.0 27.6 %all-to-all-start.1 = ((bf16[4,25,32,128]{3,2,1,0:T(8,128)(2,1)}), bf16[4,25,32,128]{3,2,1,0:T(8,128)(2,1)S(1)}, u32[]{:S(2)}, u32[]{:S(2)}) async-start(bf16[4,25,32,128]{3,2,1,0:T(8,128)(2,1)} %copy-done.7), calls=%async_computation.1 | async-start | bytes 1638400 | tf_op jit(solution)/shard_map/all_to_all | solution.py:395
  71.2 2.5 %copy-start.1 = (f32[4,4,128,640]{3,2,1,0:T(8,128)S(1)}, f32[4,4,128,640]{3,2,1,0:T(8,128)}, u32[]{:S(2)}) copy-start(f32[4,4,128,640]{3,2,1,0:T(8,128)} %copy-done) | copy-start | bytes 15728644
  73.7 1.4 %copy-start.5 = (bf16[8,4,200,128]{3,2,1,0:T(8,128)(2,1)S(1)}, bf16[8,4,200,128]{3,2,1,0:T(8,128)(2,1)}, u32[]{:S(2)}) copy-start(bf16[8,4,200,128]{3,2,1,0:T(8,128)(2,1)} %copy-done.4) | copy-start | bytes 4915204
  79.6 4.0 %collective-permute-start.4 = (f32[2,3,128]{2,1,0:T(4,128)S(1)}, f32[2,3,128]{2,1,0:T(4,128)S(1)}, u32[]{:S(2)}, u32[]{:S(2)}) collective-permute-start(f32[2,3,128]{2,1,0:T(4,128)S(1)} %get-tuple-element.12), channel_id=1, source_target_pairs={{0,4},{4,8},{8,12},{12,16},{16,20},{20,24},{24,28},{28,0},{1,5},{5... | collective-permute-start | bytes 9224 | tf_op jit(solution)/shard_map/ppermute | solution.py:397
  81.2 2.5 %collective-permute-start.5 = (f32[2,3,128]{2,1,0:T(4,128)S(1)}, f32[2,3,128]{2,1,0:T(4,128)S(1)}, u32[]{:S(2)}, u32[]{:S(2)}) collective-permute-start(f32[2,3,128]{2,1,0:T(4,128)S(1)} %get-tuple-element.13), channel_id=1, source_target_pairs={{4,0},{8,4},{12,8},{16,12},{20,16},{24,20},{28,24},{0,28},{5,1},{9... | collective-permute-start | bytes 9224 | tf_op jit(solution)/shard_map/ppermute | solution.py:396
  83.7 5.9 %collective-permute-start.6 = (f32[3,128]{1,0:T(4,128)S(1)}, f32[3,128]{1,0:T(4,128)S(1)}, u32[]{:S(2)}, u32[]{:S(2)}) collective-permute-start(f32[3,128]{1,0:T(4,128)S(1)} %get-tuple-element.14), channel_id=1, source_target_pairs={{0,1},{1,2},{2,3},{3,0},{4,5},{5,6},{6,7},{7,4},{8,9},{9,10},{10,1... | collective-permute-start | bytes 4616 | tf_op jit(solution)/shard_map/ppermute | solution.py:404
  85.7 7.3 %collective-permute-start.7 = (f32[3,128]{1,0:T(4,128)S(1)}, f32[3,128]{1,0:T(4,128)S(1)}, u32[]{:S(2)}, u32[]{:S(2)}) collective-permute-start(f32[3,128]{1,0:T(4,128)S(1)} %get-tuple-element.16), channel_id=1, source_target_pairs={{0,2},{1,3},{2,0},{3,1},{4,6},{5,7},{6,4},{7,5},{8,10},{9,11},{10,... | collective-permute-start | bytes 4616 | tf_op jit(solution)/shard_map/ppermute | solution.py:404
  88.1 4.9 %collective-permute-start.8 = (f32[3,128]{1,0:T(4,128)S(1)}, f32[3,128]{1,0:T(4,128)S(1)}, u32[]{:S(2)}, u32[]{:S(2)}) collective-permute-start(f32[3,128]{1,0:T(4,128)S(1)} %get-tuple-element.15), channel_id=1, source_target_pairs={{0,3},{1,0},{2,1},{3,2},{4,7},{5,4},{6,5},{7,6},{8,11},{9,8},{10,9... | collective-permute-start | bytes 4616 | tf_op jit(solution)/shard_map/ppermute | solution.py:404

commit v3 on v1

v3 whole, which is shorter than its diff:
```python
import functools
import math

import jax
import jax.numpy as jnp
from jax import lax
from jax.experimental import pallas as pl
from jax.experimental.pallas import tpu as pltpu
from jax.sharding import PartitionSpec as P

BLOCK = 64
REACH = 4
FAR = 1e30
VMEM_LIMIT = 40 * 1024 * 1024


def degree_of(k):
    return math.isqrt(k)


def pair_table(comp):
    pairs = []
    for k in range(comp):
        l = degree_of(k)
        for m in range(l * l, (l + 1) * (l + 1)):
            pairs.append((k, m))
    return pairs


def vmem():
    return pl.BlockSpec(memory_space=pltpu.VMEM)


def dot(a, b, ca, cb):
    return lax.dot_general(
        a, b, (((ca,), (cb,)), ((), ())), preferred_element_type=jnp.float32
    )


def rotated_rows(coef, tile, comp, source, k, turned):
    index_of = {pair: n for n, pair in enumerate(pair_table(comp))}
    l = degree_of(k)
    total = None
    for m in range(l * l, (l + 1) * (l + 1)):
        row = index_of[(m, k) if turned else (k, m)]
        term = coef[tile, row : row + 1, :] * source(m)
        total = term if total is None else total + term
    return total


def fused_kernel(
    heads,
    alpha,
    doms,
    ranks,
    halo,
    penalty,
    frame_index,
    neighbours,
    counts,
    features,
    cotangent,
    value_weight,
    output_weight,
    q_weight,
    k_weight,
    frames,
    own_points,
    updated,
    force,
    packed,
    ext,
    grads,
    back,
    finished,
    arrived,
    points,
    points_t,
    coef,
    mask,
    values_s,
    keys_s,
    queries_s,
    rotated_s,
    aggregate_s,
    attention_s,
    forces,
    from_low,
    from_high,
    shared,
    shares,
    value_sems,
    back_sems,
    finished_sems,
    share_sems,
    halo_sems,
    point_sems,
    rim_sems,
):
    comp, channels, atoms = features.shape
    tiles = own_points.shape[0]
    width = channels // ranks
    head_width = width // heads
    slots = tiles + 2 * halo
    window = 2 * halo + 1
    per_tile = atoms // BLOCK
    me = lax.axis_index("head")
    dom = lax.axis_index("dom")
    up = lax.rem(dom + 1, doms)
    down = lax.rem(dom + doms - 1, doms)

    def peer(shift):
        return lax.rem(me + shift, ranks)

    def source(shift):
        return lax.rem(me + ranks - shift, ranks)

    def remote(src, dst, sems, at, device):
        return pltpu.make_async_remote_copy(
            src_ref=src,
            dst_ref=dst,
            send_sem=sems.at[0, at],
            recv_sem=sems.at[1, at],
            device_id=device,
            device_id_type=pl.DeviceIdType.MESH,
        )

    barrier = pltpu.get_barrier_semaphore()
    for shift in range(1, ranks):
        pl.semaphore_signal(
            barrier, inc=1, device_id=(dom, peer(shift)), device_id_type=pl.DeviceIdType.MESH
        )
    for side in (up, down):
        pl.semaphore_signal(
            barrier, inc=1, device_id=(side, me), device_id_type=pl.DeviceIdType.MESH
        )

    for k in range(comp):
        mixed = dot(value_weight[degree_of(k)], features[k], 0, 0)
        packed[:, k] = mixed.reshape(ranks, width, atoms).astype(jnp.bfloat16)
    scalars = features[0].astype(jnp.float32).reshape(ranks, width, atoms).astype(jnp.bfloat16)
    for r in range(ranks):
        packed[r, comp:] = scalars

    pl.semaphore_wait(barrier, ranks + 1)

    value_copies = [
        remote(packed.at[peer(r)], ext.at[halo + me], value_sems, r, (dom, peer(r)))
        for r in range(1, ranks)
    ]
    for copy in value_copies:
        copy.start()
    point_copies = [
        remote(
            own_points.at[pl.ds(tiles - halo, halo)], points.at[pl.ds(0, halo)], point_sems, 0, (up, me)
        ),
        remote(
            own_points.at[pl.ds(0, halo)],
            points.at[pl.ds(halo + tiles, halo)],
            point_sems,
            1,
            (down, me),
        ),
    ]
    for copy in point_copies:
        copy.start()

    for k in range(comp):
        mixed = dot(output_weight[degree_of(k)], cotangent[k], 1, 0)
        grads[:, k] = mixed.reshape(ranks, width, atoms).astype(jnp.bfloat16)
    ext[halo + me] = packed[me]
    back[me] = grads[me]
    points[halo : halo + tiles] = own_points[...]

    components = lax.broadcasted_iota(jnp.int32, (comp, 1), 0)
    degrees = jnp.zeros_like(components)
    for l in range(1, degree_of(comp - 1) + 1):
        degrees = degrees + (components >= l * l).astype(jnp.int32)
    keep = (jnp.abs(components - degrees * degrees - degrees) <= 2).astype(jnp.float32)
    blocks = tiles * per_tile
    lane = lax.broadcasted_iota(jnp.int32, (1, atoms), 1)
    slot_of = lax.broadcasted_iota(jnp.int32, (1, window * atoms), 1) // BLOCK

    def tables(t, carry):
        points_t[t] = own_points[t].T
        matrices = []
        for r in range(per_tile):
            frame = frames[frame_index[t * per_tile + r]]
            matrices.append(
                lax.dot_general(
                    frame * keep,
                    frame,
                    (((0,), (0,)), ((), ())),
                    precision=lax.Precision.HIGHEST,
                    preferred_element_type=jnp.float32,
                )
            )
        at = 0
        for k in range(comp):
            l = degree_of(k)
            first, last = l * l, (l + 1) * (l + 1)
            rows = jnp.broadcast_to(matrices[0][first:last, k : k + 1], (last - first, atoms))
            for r in range(1, per_tile):
                here = jnp.broadcast_to(matrices[r][first:last, k : k + 1], (last - first, atoms))
                rows = jnp.where(lane < r * BLOCK, rows, here)
            coef[t, at : at + last - first, :] = rows
            at += last - first
        for r in range(per_tile):
            block = t * per_tile + r
            hidden = jnp.full((1, window * atoms), FAR, jnp.float32)
            shift = r + halo * per_tile - REACH
            for s in range(neighbours.shape[1]):
                offset = lax.rem(
                    neighbours[block, s] - (dom * blocks + block) + REACH + doms * blocks,
                    doms * blocks,
                )
                place = jnp.where(counts[block] > s, offset + shift, -1)
                hidden = jnp.where(slot_of == place, 0.0, hidden)
            mask[t, r : r + 1, :] = hidden
        return carry

    lax.fori_loop(0, tiles, tables, 0)

    for r in range(1, ranks):
        remote(packed.at[peer(r)], ext.at[halo + source(r)], value_sems, r, (dom, peer(r))).wait_recv()
    halo_copies = [
        remote(ext.at[pl.ds(tiles, halo)], ext.at[pl.ds(0, halo)], halo_sems, 0, (up, me)),
        remote(
            ext.at[pl.ds(halo, halo)], ext.at[pl.ds(halo + tiles, halo)], halo_sems, 1, (down, me)
        ),
    ]
    for copy in halo_copies:
        copy.start()
    back_copies = [
        remote(grads.at[peer(r)], back.at[me], back_sems, r, (dom, peer(r)))
        for r in range(1, ranks)
    ]
    for copy in back_copies:
        copy.start()

    def prepare(slot, with_query):
        tile = ext[slot].astype(jnp.float32)
        for h in range(heads):
            part = tile[:comp, h * head_width : (h + 1) * head_width]
            values_s[slot, h] = part.reshape(comp * head_width, atoms).astype(jnp.bfloat16)
        scalars = tile[comp:].reshape(channels, atoms)
        keys = dot(k_weight[...], scalars.astype(jnp.bfloat16), 0, 0)
        keys_s[slot] = keys.reshape(heads, alpha, atoms).astype(jnp.bfloat16)
        if with_query:
            turned = scalars.T.astype(jnp.bfloat16)
            for h in range(heads):
                queries_s[slot - halo, h] = dot(
                    turned, q_weight[:, h * alpha : (h + 1) * alpha], 1, 0
                ).astype(jnp.bfloat16)

    def inner(i, carry):
        prepare(i + halo, True)
        return carry

    lax.fori_loop(0, tiles, inner, 0)
    for copy in halo_copies + point_copies:
        copy.wait_recv()

    def edge(i, carry):
        prepare(i, False)
        prepare(i + halo + tiles, False)
        return carry

    lax.fori_loop(0, halo, edge, 0)

    def windowed(t, get):
        return jnp.concatenate([get(t + w) for w in range(window)], axis=-1)

    scale = 1.0 / math.sqrt(alpha)

    def send_finished(i):
        return remote(
            finished.at[peer(i)], arrived.at[me], finished_sems, i, (dom, peer(i))
        )

    def gather(i, carry):
        t = peer(i + 1)
        distance = None
        for c in range(3):
            row = windowed(t, lambda s: points[s, c : c + 1, :])
            apart = points_t[t, :, c : c + 1] - row
            distance = apart * apart if distance is None else distance + apart * apart
        hidden = jnp.concatenate(
            [
                jnp.broadcast_to(mask[t, r : r + 1, :], (BLOCK, window * atoms))
                for r in range(per_tile)
            ],
            axis=0,
        )
        distance = jnp.maximum(distance, hidden)

        @pl.when(i >= 1)
        def _():
            send_finished(i).start()

        for h in range(heads):
            keys = windowed(t, lambda s: keys_s[s, h])
            values = windowed(t, lambda s: values_s[s, h])
            strength = penalty[me * heads + h]
            logits = dot(queries_s[t, h], keys, 1, 0) * scale - strength * distance
            peaks = jnp.max(logits, axis=1, keepdims=True)
            exponent = jnp.exp(logits - peaks)
            inverse = 1.0 / jnp.sum(exponent, axis=1, keepdims=True)
            attention = exponent * inverse
            attention_s[t, h] = attention
            aggregate = dot(values, attention.astype(jnp.bfloat16), 1, 1)
            aggregate_s[:, h * head_width : (h + 1) * head_width] = aggregate.reshape(
                comp, head_width, atoms
            )
        for k in range(comp):
            finished[t, k] = rotated_rows(
                coef, t, comp, lambda m: aggregate_s[m], k, False
            ).astype(jnp.bfloat16)
        return carry

    lax.fori_loop(0, ranks, gather, 0)
    arrived[me] = finished[me]

    forces[...] = jnp.zeros_like(forces)
    for r in range(1, ranks):
        remote(grads.at[peer(r)], back.at[source(r)], back_sems, r, (dom, peer(r))).wait_recv()

    lane_square = lax.broadcasted_iota(jnp.int32, (atoms, atoms), 1)

    def terms(t, carry):
        for k in range(comp):
            rotated_s[k] = (
                rotated_rows(coef, t, comp, lambda m: back[t, m].astype(jnp.float32), k, True)
                .astype(jnp.bfloat16)
                .astype(jnp.float32)
            )
        total = jnp.zeros((atoms, window * atoms), jnp.float32)
        for h in range(heads):
            values = windowed(t, lambda s: values_s[s, h])
            attention = attention_s[t, h]
            turned = rotated_s[:, h * head_width : (h + 1) * head_width].reshape(
                comp * head_width, atoms
            )
            weight_grads = dot(turned.T.astype(jnp.bfloat16), values, 1, 0)
            mean = jnp.sum(attention * weight_grads, axis=1, keepdims=True)
            strength = penalty[me * heads + h]
            total = total + (2.0 * strength) * (attention * (weight_grads - mean))
        mine = jnp.zeros((atoms, atoms), jnp.float32)
        theirs = []
        for c in range(3):
            row = windowed(t, lambda s: points[s, c : c + 1, :])
            weighted = total * (points_t[t, :, c : c + 1] - row)
            mine = jnp.where(lane_square == c, jnp.sum(weighted, axis=1, keepdims=True), mine)
            theirs.append(jnp.sum(weighted, axis=0, keepdims=True))
        mine = mine.T
        for c in range(3):
            forces[t + halo, c : c + 1, :] = forces[t + halo, c : c + 1, :] + mine[c : c + 1]
            for w in range(window):
                forces[t + w, c : c + 1, :] = (
                    forces[t + w, c : c + 1, :] - theirs[c][:, w * atoms : (w + 1) * atoms]
                )
        return carry

    lax.fori_loop(0, tiles, terms, 0)

    rim_copies = [
        remote(forces.at[pl.ds(halo + tiles, halo)], from_low, rim_sems, 0, (up, me)),
        remote(forces.at[pl.ds(0, halo)], from_high, rim_sems, 1, (down, me)),
    ]
    for copy in rim_copies:
        copy.start()
    for copy in value_copies + halo_copies + point_copies + back_copies:
        copy.wait_send()
    for copy in rim_copies:
        copy.wait_recv()
    shared[...] = forces[halo : halo + tiles]
    shared[:halo] = shared[:halo] + from_low[...]
    shared[tiles - halo :] = shared[tiles - halo :] + from_high[...]
    shares[me] = shared[me]
    share_copies = [
        remote(shared.at[peer(r)], shares.at[me], share_sems, r, (dom, peer(r)))
        for r in range(1, ranks)
    ]
    for copy in share_copies:
        copy.start()

    for r in range(1, ranks):
        remote(
            finished.at[peer(r)], arrived.at[source(r)], finished_sems, r, (dom, peer(r))
        ).wait_recv()
    for k in range(comp):
        gathered = arrived[:, k].astype(jnp.float32).reshape(channels, atoms)
        mixed = dot(output_weight[degree_of(k)], gathered.astype(jnp.bfloat16), 0, 0)
        updated[k] = (features[k].astype(jnp.float32) + mixed).astype(jnp.bfloat16)

    for r in range(1, ranks):
        remote(
            shared.at[peer(r)], shares.at[source(r)], share_sems, r, (dom, peer(r))
        ).wait_recv()
    summed = shares[0]
    for r in range(1, ranks):
        summed = summed + shares[r]
    force[...] = summed[:3]
    for copy in rim_copies + share_copies:
        copy.wait_send()
    for r in range(1, ranks):
        send_finished(r).wait_send()


def on_device(
    features,
    positions,
    penalty,
    qk_weight,
    value_weight,
    output_weight,
    frames,
    frame_index,
    neighbours,
    counts,
    cotangent,
):
    comp, channels, atoms = features.shape
    ranks = lax.axis_size("head")
    doms = lax.axis_size("dom")
    heads_all = penalty.shape[0]
    heads = heads_all // ranks
    alpha = qk_weight.shape[1] // (2 * heads_all)
    width = channels // ranks
    tiles = positions.shape[1] // atoms
    per_tile = atoms // BLOCK
    halo = -(-REACH * BLOCK // atoms)
    window = 2 * halo + 1
    scalar_rows = channels // width
    head_width = width // heads
    slots = tiles + 2 * halo
    rank = lax.axis_index("head")
    table_rows = len(pair_table(comp))

    padded = jnp.pad(positions, ((0, 8 - positions.shape[0]), (0, 0)))
    own_points = padded.reshape(8, tiles, atoms).transpose(1, 0, 2)
    q_weight = lax.dynamic_slice_in_dim(qk_weight, rank * heads * alpha, heads * alpha, 1)
    k_weight = lax.dynamic_slice_in_dim(
        qk_weight, (heads_all + rank * heads) * alpha, heads * alpha, 1
    )
    bf16, f32 = jnp.bfloat16, jnp.float32
    smem = pl.BlockSpec(memory_space=pltpu.SMEM)
    dma = pltpu.SemaphoreType.DMA
    return pl.pallas_call(
        functools.partial(fused_kernel, heads, alpha, doms, ranks, halo),
        out_shape=(
            jax.ShapeDtypeStruct(features.shape, bf16),
            jax.ShapeDtypeStruct((positions.shape[0], atoms), f32),
        ),
        in_specs=[smem] * 4 + [vmem()] * 8,
        out_specs=(vmem(), vmem()),
        scratch_shapes=[
            pltpu.VMEM((ranks, comp + scalar_rows, width, atoms), bf16),
            pltpu.VMEM((slots, comp + scalar_rows, width, atoms), bf16),
            pltpu.VMEM((ranks, comp, width, atoms), bf16),
            pltpu.VMEM((tiles, comp, width, atoms), bf16),
            pltpu.VMEM((tiles, comp, width, atoms), bf16),
            pltpu.VMEM((ranks, comp, width, atoms), bf16),
            pltpu.VMEM((slots, 8, atoms), f32),
            pltpu.VMEM((tiles, atoms, 8), f32),
            pltpu.VMEM((tiles, table_rows, atoms), f32),
            pltpu.VMEM((tiles, per_tile, window * atoms), f32),
            pltpu.VMEM((slots, heads, comp * head_width, atoms), bf16),
            pltpu.VMEM((slots, heads, alpha, atoms), bf16),
            pltpu.VMEM((tiles, heads, atoms, alpha), bf16),
            pltpu.VMEM((comp, width, atoms), f32),
            pltpu.VMEM((comp, width, atoms), f32),
            pltpu.VMEM((tiles, heads, atoms, window * atoms), f32),
            pltpu.VMEM((slots, 8, atoms), f32),
            pltpu.VMEM((halo, 8, atoms), f32),
            pltpu.VMEM((halo, 8, atoms), f32),
            pltpu.VMEM((tiles, 8, atoms), f32),
            pltpu.VMEM((ranks, 8, atoms), f32),
            dma((2, ranks)),
            dma((2, ranks)),
            dma((2, ranks)),
            dma((2, ranks)),
            dma((2, 2)),
            dma((2, 2)),
            dma((2, 2)),
        ],
        compiler_params=pltpu.CompilerParams(
            vmem_limit_bytes=VMEM_LIMIT, collective_id=0, has_side_effects=True
        ),
        name="layer",
    )(
        penalty,
        frame_index,
        neighbours,
        counts,
        features,
        cotangent,
        value_weight,
        output_weight,
        q_weight,
        k_weight,
        frames,
        own_points,
    )


def solution(mesh):
    split = ("dom", "head")
    in_specs = (
        P(None, None, split),
        P(None, "dom"),
        P(),
        P(),
        P(),
        P(),
        P(),
        P("dom"),
        P("dom", None),
        P("dom"),
        P(None, None, split),
    )
    out_specs = (P(None, None, split), P(None, split))
    return jax.shard_map(
        on_device, mesh=mesh, in_specs=in_specs, out_specs=out_specs, check_vma=False
    )
```

time: 113 us -> 73.4 us (0.65)
  Pallas kernels: 17.6 us -> 64.9 us
  waiting for transfers between devices: 41.5 us -> 0 us
  starting transfers between devices: 21.5 us -> 0 us
  local copies, waits for them, and re-layouts: 19.5 us -> 7 us
  blocking collectives: 8.11 us -> 0 us
  other arithmetic: 2.78 us -> 0 us
    pallas_call x4 -> x1, Pallas kernels: 17.6 us -> 64.9 us  [on_device(): pl.pallas_call(functools.partial(fused_kernel, heads, alpha, doms, ranks,...]
    all_to_all x3 -> x0, waiting for transfers between devices: 40.1 us -> none  [the longest x1 20 us: on_device(): lax.all_to_all(attended, 'head', split_axis=0, concat_axis=0, tiled=True)]
    all_to_all x3 -> x0, starting transfers between devices: 13.6 us -> none  [the longest x1 6.48 us: on_device(): lax.all_to_all(packed, 'head', split_axis=0, concat_axis=0, tiled=True)]
    all_to_all x1 -> x0, blocking collectives: 8.11 us -> none  [on_device(): lax.all_to_all(shared, 'head', split_axis=0, concat_axis=0, tiled=True)]
    ppermute x6 -> x0, starting transfers between devices: 7.93 us -> none  [the longest x1 2.64 us: on_device(): low = lax.ppermute(forces[:halo], 'dom', down)]
    gather x4 -> x0, local copies, waits for them, and re-layouts: 4.16 us -> none  [the longest x3 2.37 us: on_device(): jnp.take(flat, jnp.asarray(pairs[:, 0] * comp + pairs[:, 1]), axis=1)]
    reshape x4 -> x0, local copies, waits for them, and re-layouts: 2.21 us -> none  [the longest x1 1.23 us: on_device(): coef = jnp.broadcast_to(picked.reshape(tiles, per_tile, -1).transpose(0,...]
    unnamed x34 -> x21, local copies, waits for them, and re-layouts: 7.79 us -> 5.99 us
  transfers between devices with their start and end apart: 9 -> 0, of which waited for: 4 -> 0; matrix products, arithmetic and copies ran while one was open for 15% -> 0% of each run, Pallas kernels for 1% -> 0%
where the time goes in v3:
time: 73.4 us; the launch traced here: 72.6 us
  Pallas kernels  64.9 us (88%)
  local copies, waits for them, and re-layouts  7 us (10%)
  between operations  0.76 us (1%)
    pallas_call x1, Pallas kernels, on_device(): pl.pallas_call(functools.partial(fused_kernel, heads, alpha, doms, ranks,...  64.9 us
    unnamed x21, local copies, waits for them, and re-layouts  5.99 us

profile of v3, /device:TPU:0, one launch (start us, length us, event | category | flops | bytes accessed | tf_op | source)
XLA Modules:
  0.0 72.6 jit_solution(17281080213557120519)
XLA Ops:
  0.6 0.0 copy-start.8
  0.6 0.7 copy-done.8
  1.3 0.0 copy-start
  1.3 0.0 copy-start.1
  1.3 1.0 %constant_dynamic-slice_fusion = (bf16[128,256]{1,0:T(8,128)(2,1)S(1)}, bf16[128,256]{1,0:T(8,128)(2,1)S(1)}) fusion(bf16[128,2048]{1,0:T(8,128)(2,1)} %param.14, s32[]{:T(128)S(6)} %select_n.7, s32[]{:T(128)S(6)} %select_n.6), kind=kLoop, calls=%fused_computation.1 | loop fusion | bytes 262152 | tf_op jit(solution)/shard_map/dynamic_slice | solution.py:443
  2.3 0.0 copy-start.4
  2.4 0.0 copy-start.5
  2.4 0.0 copy-start.6
  2.4 0.0 copy-start.7
  2.4 2.0 %copy.13.frames = f32[64,25,25]{2,1,0:T(8,128)S(1)} copy(f32[64,25,25]{0,2,1:T(8,128)} %param.17) | data formatting | bytes 320000 | tf_op args[6]
  4.4 0.0 copy-done
  4.4 0.0 copy-done.1
  4.4 0.0 copy-done.4
  4.4 0.0 copy-done.5
  4.4 0.0 copy-done.6
  4.4 0.0 copy-done.7
  4.4 0.0 copy-start.2
  4.4 0.9 %copy-done.2 = bf16[5,128,128]{2,1,0:T(8,128)(2,1)S(1)} copy-done((bf16[5,128,128]{2,1,0:T(8,128)(2,1)S(1)}, bf16[5,128,128]{2,1,0:T(8,128)(2,1)}, u32[]{:S(2)}) %copy-start.2) | copy-done | bytes 163864
  5.4 0.0 copy-start.3
  5.4 0.9 %copy-done.3 = bf16[5,128,128]{2,1,0:T(8,128)(2,1)S(1)} copy-done((bf16[5,128,128]{2,1,0:T(8,128)(2,1)S(1)}, bf16[5,128,128]{2,1,0:T(8,128)(2,1)}, u32[]{:S(2)}) %copy-start.3) | copy-done | bytes 163864
  6.3 64.9 %layer.1 = (bf16[25,128,128]{2,1,0:T(8,128)(2,1)S(1)}, f32[3,128]{1,0:T(4,128)S(1)}) custom-call(f32[16]{0:T(128)S(1)} %copy-done.5, s32[8]{0:T(128)S(1)} %copy-done.6, s32[8,8]{1,0:T(8,128)S(1)} %copy-done.4, s32[8]{0:T(128)S(1)} %copy-done.7, bf16[25,128,128]{2,1,0:T(8,128)(2,1)S(1)} %copy-done, bf16[25,128,128]{2,1,0:T(8,128)(2,1)S(1)} %copy-done.1, ...), custom_call_target="tpu_custom_call" | custom-call | tf_op jit(solution)/shard_map/layer/pallas_call | solution.py:449
  71.1 0.9 %copy.16 = bf16[25,128,128]{2,1,0:T(8,128)(2,1)} copy(bf16[25,128,128]{2,1,0:T(8,128)(2,1)S(1)} %get-tuple-element.6) | data formatting | bytes 1638400
  72.0 0.6 copy.17
  (1 shorter events, 0.0 us)
Async XLA Ops:
  0.6 0.7 copy-start.8
  1.3 3.0 %copy-start = (bf16[25,128,128]{2,1,0:T(8,128)(2,1)S(1)}, bf16[25,128,128]{2,1,0:T(8,128)(2,1)}, u32[]{:S(2)}) copy-start(bf16[25,128,128]{2,1,0:T(8,128)(2,1)} %features.1) | copy-start | bytes 2457604
  1.3 3.1 %copy-start.1 = (bf16[25,128,128]{2,1,0:T(8,128)(2,1)S(1)}, bf16[25,128,128]{2,1,0:T(8,128)(2,1)}, u32[]{:S(2)}) copy-start(bf16[25,128,128]{2,1,0:T(8,128)(2,1)} %cotangent.1) | copy-start | bytes 2457604
  2.3 2.1 %copy-start.4 = (s32[8,8]{1,0:T(8,128)S(1)}, s32[8,8]{1,0:T(8,128)}, u32[]{:S(2)}) copy-start(s32[8,8]{1,0:T(8,128)} %neighbours.1) | copy-start | bytes 772
  2.4 2.1 %copy-start.5 = (f32[16]{0:T(128)S(1)}, f32[16]{0:T(128)}, u32[]{:S(2)}) copy-start(f32[16]{0:T(128)} %penalty.1) | copy-start | bytes 196
  2.4 2.0 %copy-start.6 = (s32[8]{0:T(128)S(1)}, s32[8]{0:T(128)}, u32[]{:S(2)}) copy-start(s32[8]{0:T(128)} %frame_index.1) | copy-start | bytes 100
  2.4 2.0 %copy-start.7 = (s32[8]{0:T(128)S(1)}, s32[8]{0:T(128)}, u32[]{:S(2)}) copy-start(s32[8]{0:T(128)} %counts.1) | copy-start | bytes 100
  4.4 0.9 %copy-start.2 = (bf16[5,128,128]{2,1,0:T(8,128)(2,1)S(1)}, bf16[5,128,128]{2,1,0:T(8,128)(2,1)}, u32[]{:S(2)}) copy-start(bf16[5,128,128]{2,1,0:T(8,128)(2,1)} %value_weight.1) | copy-start | bytes 491524
  5.4 0.9 %copy-start.3 = (bf16[5,128,128]{2,1,0:T(8,128)(2,1)S(1)}, bf16[5,128,128]{2,1,0:T(8,128)(2,1)}, u32[]{:S(2)}) copy-start(bf16[5,128,128]{2,1,0:T(8,128)(2,1)} %output_weight.1) | copy-start | bytes 491524

commit v4 on v3

--- a/solution.py
+++ b/solution.py
@@ -11,7 +11,7 @@
 BLOCK = 64
 REACH = 4
 FAR = 1e30
-VMEM_LIMIT = 40 * 1024 * 1024
+VMEM_LIMIT = 63 * 1024 * 1024
 
 
 def degree_of(k):
@@ -58,14 +58,13 @@
     frame_index,
     neighbours,
     counts,
-    features,
-    cotangent,
-    value_weight,
-    output_weight,
-    q_weight,
-    k_weight,
-    frames,
-    own_points,
+    features_in,
+    cotangent_in,
+    value_weight_in,
+    output_weight_in,
+    qk_weight_in,
+    frames_in,
+    positions_in,
     updated,
     force,
     packed,
@@ -96,6 +95,17 @@
     halo_sems,
     point_sems,
     rim_sems,
+    features,
+    cotangent,
+    value_weight,
+    output_weight,
+    qk_weight,
+    frames,
+    positions,
+    q_weight,
+    k_weight,
+    own_points,
+    load_sems,
 ):
     comp, channels, atoms = features.shape
     tiles = own_points.shape[0]
@@ -109,6 +119,23 @@
     up = lax.rem(dom + 1, doms)
     down = lax.rem(dom + doms - 1, doms)
 
+    loads = [
+        pltpu.make_async_copy(src, dst, load_sems.at[n])
+        for n, (src, dst) in enumerate(
+            [
+                (features_in, features),
+                (value_weight_in, value_weight),
+                (positions_in, positions),
+                (cotangent_in, cotangent),
+                (output_weight_in, output_weight),
+                (frames_in, frames),
+                (qk_weight_in, qk_weight),
+            ]
+        )
+    ]
+    for load in loads:
+        load.start()
+
     def peer(shift):
         return lax.rem(me + shift, ranks)
 
@@ -135,6 +162,11 @@
             barrier, inc=1, device_id=(side, me), device_id_type=pl.DeviceIdType.MESH
         )
 
+    for load in loads[:3]:
+        load.wait()
+    own_points[...] = jnp.zeros_like(own_points)
+    for t in range(tiles):
+        own_points[t, : positions.shape[0]] = positions[:, t * atoms : (t + 1) * atoms]
     for k in range(comp):
         mixed = dot(value_weight[degree_of(k)], features[k], 0, 0)
         packed[:, k] = mixed.reshape(ranks, width, atoms).astype(jnp.bfloat16)
@@ -165,6 +197,8 @@
     for copy in point_copies:
         copy.start()
 
+    for load in loads[3:]:
+        load.wait()
     for k in range(comp):
         mixed = dot(output_weight[degree_of(k)], cotangent[k], 1, 0)
         grads[:, k] = mixed.reshape(ranks, width, atoms).astype(jnp.bfloat16)
@@ -172,39 +206,49 @@
     back[me] = grads[me]
     points[halo : halo + tiles] = own_points[...]
 
-    components = lax.broadcasted_iota(jnp.int32, (comp, 1), 0)
-    degrees = jnp.zeros_like(components)
-    for l in range(1, degree_of(comp - 1) + 1):
-        degrees = degrees + (components >= l * l).astype(jnp.int32)
-    keep = (jnp.abs(components - degrees * degrees - degrees) <= 2).astype(jnp.float32)
+    head_columns = heads * alpha
+    span = max(head_columns, 128)
+    for part, target in enumerate((q_weight, k_weight)):
+        at = part * ranks * head_columns + lax.div(me * head_columns, span) * span
+        columns = qk_weight[:, pl.ds(pl.multiple_of(at, 128), span)]
+        picked = columns[:, :head_columns]
+        for n in range(1, span // head_columns):
+            here = columns[:, n * head_columns : (n + 1) * head_columns]
+            picked = jnp.where(lax.rem(me, span // head_columns) == n, here, picked)
+        target[...] = picked
+
     blocks = tiles * per_tile
-    lane = lax.broadcasted_iota(jnp.int32, (1, atoms), 1)
+    lane = lax.broadcasted_iota(jnp.int32, (frames.shape[2], atoms), 1)
+    frame_row = lax.broadcasted_iota(jnp.int32, (frames.shape[2], atoms), 0)
     slot_of = lax.broadcasted_iota(jnp.int32, (1, window * atoms), 1) // BLOCK
 
     def tables(t, carry):
         points_t[t] = own_points[t].T
-        matrices = []
-        for r in range(per_tile):
-            frame = frames[frame_index[t * per_tile + r]]
-            matrices.append(
+        wanted = jnp.zeros_like(lane) + frame_index[t * per_tile]
+        for r in range(1, per_tile):
+            wanted = jnp.where(lane < r * BLOCK, wanted, frame_index[t * per_tile + r])
+        onehot = (frame_row == wanted).astype(jnp.float32)
+        at = 0
+        for l in range(degree_of(comp - 1) + 1):
+            first, last = l * l, (l + 1) * (l + 1)
+            kept = [
                 lax.dot_general(
-                    frame * keep,
-                    frame,
-                    (((0,), (0,)), ((), ())),
+                    frames[j],
+                    onehot,
+                    (((1,), (0,)), ((), ())),
                     precision=lax.Precision.HIGHEST,
                     preferred_element_type=jnp.float32,
                 )
-            )
-        at = 0
-        for k in range(comp):
-            l = degree_of(k)
-            first, last = l * l, (l + 1) * (l + 1)
-            rows = jnp.broadcast_to(matrices[0][first:last, k : k + 1], (last - first, atoms))
-            for r in range(1, per_tile):
-                here = jnp.broadcast_to(matrices[r][first:last, k : k + 1], (last - first, atoms))
-                rows = jnp.where(lane < r * BLOCK, rows, here)
-            coef[t, at : at + last - first, :] = rows
-            at += last - first
+                for j in range(first, last)
+                if abs(j - first - l) <= 2
+            ]
+            for k in range(first, last):
+                rows = None
+                for matrix in kept:
+                    term = matrix[k : k + 1, :] * matrix[first:last, :]
+                    rows = term if rows is None else rows + term
+                coef[t, at : at + last - first, :] = rows
+                at += last - first
         for r in range(per_tile):
             block = t * per_tile + r
             hidden = jnp.full((1, window * atoms), FAR, jnp.float32)
@@ -221,6 +265,13 @@
 
     lax.fori_loop(0, tiles, tables, 0)
 
+    back_copies = [
+        remote(grads.at[peer(r)], back.at[me], back_sems, r, (dom, peer(r)))
+        for r in range(1, ranks)
+    ]
+    for copy in back_copies:
+        copy.start()
+
     for r in range(1, ranks):
         remote(packed.at[peer(r)], ext.at[halo + source(r)], value_sems, r, (dom, peer(r))).wait_recv()
     halo_copies = [
@@ -231,13 +282,6 @@
     ]
     for copy in halo_copies:
         copy.start()
-    back_copies = [
-        remote(grads.at[peer(r)], back.at[me], back_sems, r, (dom, peer(r)))
-        for r in range(1, ranks)
-    ]
-    for copy in back_copies:
-        copy.start()
-
     def prepare(slot, with_query):
         tile = ext[slot].astype(jnp.float32)
         for h in range(heads):
@@ -434,15 +478,9 @@
     scalar_rows = channels // width
     head_width = width // heads
     slots = tiles + 2 * halo
-    rank = lax.axis_index("head")
     table_rows = len(pair_table(comp))
 
-    padded = jnp.pad(positions, ((0, 8 - positions.shape[0]), (0, 0)))
-    own_points = padded.reshape(8, tiles, atoms).transpose(1, 0, 2)
-    q_weight = lax.dynamic_slice_in_dim(qk_weight, rank * heads * alpha, heads * alpha, 1)
-    k_weight = lax.dynamic_slice_in_dim(
-        qk_weight, (heads_all + rank * heads) * alpha, heads * alpha, 1
-    )
+    framed = frames.transpose(1, 2, 0)
     bf16, f32 = jnp.bfloat16, jnp.float32
     smem = pl.BlockSpec(memory_space=pltpu.SMEM)
     dma = pltpu.SemaphoreType.DMA
@@ -452,7 +490,7 @@
             jax.ShapeDtypeStruct(features.shape, bf16),
             jax.ShapeDtypeStruct((positions.shape[0], atoms), f32),
         ),
-        in_specs=[smem] * 4 + [vmem()] * 8,
+        in_specs=[smem] * 4 + [pl.BlockSpec(memory_space=pltpu.MemorySpace.HBM)] * 7,
         out_specs=(vmem(), vmem()),
         scratch_shapes=[
             pltpu.VMEM((ranks, comp + scalar_rows, width, atoms), bf16),
@@ -483,6 +521,17 @@
             dma((2, 2)),
             dma((2, 2)),
             dma((2, 2)),
+            pltpu.VMEM(features.shape, bf16),
+            pltpu.VMEM(cotangent.shape, bf16),
+            pltpu.VMEM(value_weight.shape, bf16),
+            pltpu.VMEM(output_weight.shape, bf16),
+            pltpu.VMEM(qk_weight.shape, bf16),
+            pltpu.VMEM(framed.shape, f32),
+            pltpu.VMEM(positions.shape, f32),
+            pltpu.VMEM((channels, heads * alpha), bf16),
+            pltpu.VMEM((channels, heads * alpha), bf16),
+            pltpu.VMEM((tiles, 8, atoms), f32),
+            dma((7,)),
         ],
         compiler_params=pltpu.CompilerParams(
             vmem_limit_bytes=VMEM_LIMIT, collective_id=0, has_side_effects=True
@@ -497,10 +546,9 @@
         cotangent,
         value_weight,
         output_weight,
-        q_weight,
-        k_weight,
-        frames,
-        own_points,
+        qk_weight,
+        framed,
+        positions,
     )
 
 

time: 73.4 us -> 69.9 us (0.952)
  local copies, waits for them, and re-layouts: 7 us -> 2.7 us
  Pallas kernels: 64.9 us -> 66.3 us
    unnamed x21 -> x4, local copies, waits for them, and re-layouts: 5.99 us -> 2.7 us
    pallas_call x1, Pallas kernels: 64.9 us -> 66.3 us  [on_device(): pl.pallas_call(functools.partial(fused_kernel, heads, alpha, doms, ranks,...]
    dynamic_slice x1 -> x0, local copies, waits for them, and re-layouts: 1 us -> none  [on_device(): lax.dynamic_slice_in_dim(qk_weight, (heads_all + rank * heads) * alpha, h...]
where the time goes in v4:
time: 69.9 us; the launch traced here: 69.7 us
  Pallas kernels  66.3 us (95%)
  local copies, waits for them, and re-layouts  2.7 us (4%)
    pallas_call x1, Pallas kernels, on_device(): pl.pallas_call(functools.partial(fused_kernel, heads, alpha, doms, ranks,...  66.3 us
    unnamed x4, local copies, waits for them, and re-layouts  2.7 us

profile of v4, /device:TPU:0, one launch (start us, length us, event | category | flops | bytes accessed | tf_op | source)
XLA Modules:
  0.0 69.7 jit_solution(9585711844293351221)
XLA Ops:
  0.6 66.3 %layer.1 = (bf16[25,128,128]{2,1,0:T(8,128)(2,1)}, f32[3,128]{1,0:T(4,128)}) custom-call(f32[16]{0:T(128)} %penalty.1, s32[8]{0:T(128)} %frame_index.1, s32[8,8]{1,0:T(8,128)} %neighbours.1, s32[8]{0:T(128)} %counts.1, bf16[25,128,128]{2,1,0:T(8,128)(2,1)} %features_in.1, bf16[25,128,128]{2,1,0:T(8,128)(2,1)} %cotangent_in.1, ...), custom_call_target="tpu_custom_call" | custom-call | tf_op jit(solution)/shard_map/layer/pallas_call | solution.py:487
  66.9 0.0 copy-start
  67.0 2.1 %copy.15 = bf16[25,128,128]{2,1,0:T(8,128)(2,1)} copy(bf16[25,128,128]{2,1,0:T(8,128)(2,1)} %get-tuple-element.4) | data formatting | bytes 1638400
  69.1 0.0 copy-done
  69.1 0.6 copy.16
Async XLA Ops:
  66.9 2.1 %copy-start = (f32[3,128]{1,0:T(4,128)S(1)}, f32[3,128]{1,0:T(4,128)}, u32[]{:S(2)}) copy-start(f32[3,128]{1,0:T(4,128)} %get-tuple-element.5) | copy-start | bytes 4612

commit v5 on v4

--- a/solution.py
+++ b/solution.py
@@ -265,13 +265,6 @@
 
     lax.fori_loop(0, tiles, tables, 0)
 
-    back_copies = [
-        remote(grads.at[peer(r)], back.at[me], back_sems, r, (dom, peer(r)))
-        for r in range(1, ranks)
-    ]
-    for copy in back_copies:
-        copy.start()
-
     for r in range(1, ranks):
         remote(packed.at[peer(r)], ext.at[halo + source(r)], value_sems, r, (dom, peer(r))).wait_recv()
     halo_copies = [
@@ -282,6 +275,13 @@
     ]
     for copy in halo_copies:
         copy.start()
+    back_copies = [
+        remote(grads.at[peer(r)], back.at[me], back_sems, r, (dom, peer(r)))
+        for r in range(1, ranks)
+    ]
+    for copy in back_copies:
+        copy.start()
+
     def prepare(slot, with_query):
         tile = ext[slot].astype(jnp.float32)
         for h in range(heads):

time: 69.9 us -> 70.1 us (level); the launches traced: 69.7 us -> 69 us
  no operation moved by 1% of the time
where the time goes in v5:
time: 70.1 us; the launch traced here: 69 us
  Pallas kernels  65.7 us (94%)
  local copies, waits for them, and re-layouts  2.7 us (4%)
    pallas_call x1, Pallas kernels, on_device(): pl.pallas_call(functools.partial(fused_kernel, heads, alpha, doms, ranks,...  65.7 us
    unnamed x4, local copies, waits for them, and re-layouts  2.7 us

profile of v5, /device:TPU:0, one launch (start us, length us, event | category | flops | bytes accessed | tf_op | source)
XLA Modules:
  0.0 69.0 jit_solution(6275532841653063928)
XLA Ops:
  0.6 65.7 %layer.1 = (bf16[25,128,128]{2,1,0:T(8,128)(2,1)}, f32[3,128]{1,0:T(4,128)}) custom-call(f32[16]{0:T(128)} %penalty.1, s32[8]{0:T(128)} %frame_index.1, s32[8,8]{1,0:T(8,128)} %neighbours.1, s32[8]{0:T(128)} %counts.1, bf16[25,128,128]{2,1,0:T(8,128)(2,1)} %features_in.1, bf16[25,128,128]{2,1,0:T(8,128)(2,1)} %cotangent_in.1, ...), custom_call_target="tpu_custom_call" | custom-call | tf_op jit(solution)/shard_map/layer/pallas_call | solution.py:487
  66.3 0.0 copy-start
  66.3 2.1 %copy.15 = bf16[25,128,128]{2,1,0:T(8,128)(2,1)} copy(bf16[25,128,128]{2,1,0:T(8,128)(2,1)} %get-tuple-element.4) | data formatting | bytes 1638400
  68.5 0.0 copy-done
  68.5 0.6 copy.16
Async XLA Ops:
  66.3 2.1 %copy-start = (f32[3,128]{1,0:T(4,128)S(1)}, f32[3,128]{1,0:T(4,128)}, u32[]{:S(2)}) copy-start(f32[3,128]{1,0:T(4,128)} %get-tuple-element.5) | copy-start | bytes 4612
